TPU v7x, 256 devices: a whole 4x4x8 slice. The times are simulated.
256 devices in a mesh: gx: 32 (over x_lo, z, core), gy: 8 (over x_hi, y).
Axes of the slice: x: 4 (x_hi: 2, x_lo: 2; x = x_hi * 2 + x_lo), y: 4, z: 8, core: 2. Of those that a mesh axis runs over, the one named last changes fastest.
Arguments:
- temp_adjoint: float32 [8, 1024, 4096], P(None, 'gy', 'gx'), may hold values from -6 to 6
- height_adjoint: float32 [1024, 4096], P('gy', 'gx'), may hold values from -6 to 6
- east_velocity: float32 [8, 1024, 4096], P(None, 'gy', 'gx'), may hold values from -0.8 to 0.8
- north_velocity: float32 [8, 1024, 4096], P(None, 'gy', 'gx'), may hold values from -0.8 to 0.8
- temp_store: float32 [8, 1024, 4096], P(None, 'gy', 'gx'), may hold values from -4 to 4
- salt_store: float32 [8, 1024, 4096], P(None, 'gy', 'gx'), may hold values from -4 to 4
- slot_map: int32 [32, 8, 8], P('gx', 'gy'), may hold values from 0 to 7, each once within a row
- land_mask: int32 [8, 1024, 4096], P(None, 'gy', 'gx'), may hold values 0 or 1
- ocean_depth: float32 [1024, 4096], P('gy', 'gx'), may hold values from 0.1 to 1
Outputs:
- temp_back: float32 [8, 1024, 4096], P(None, 'gy', 'gx')
- salt_back: float32 [8, 1024, 4096], P(None, 'gy', 'gx')
- surface_adjoint: float32 [1024, 4096], P('gy', 'gx')
Inputs may be any that keep to these rules, and one draw needn't show every extreme that they name: `slot_map`: each tile's entries over the last dimension name every slot 0 to 7 once.
All inputs are finite; a program needn't handle non-finite values. No bound on the sum of `land_mask` on one device may be relied on, other than what follows from the above.
Results may differ from a plain program's by a relative error of at most 0.00013.
Values sent between devices are 32-bit elements; how exact they have to be, the bound alone decides.
A program may use at most 64 MiB of HBM per device.

v0:
```python
import jax
import jax.numpy as jnp
from jax import lax
from jax.sharding import Mesh
from jax.sharding import PartitionSpec as P

ITERS = 6
GY = ("gy_0", "gy_1")
GX_GY = ("gx_0", "gx_1", "gx_2", "gy_0", "gy_1")
GX = ("gx_0", "gx_1", "gx_2")


DIFFUSE = 0.2
TIMESTEP = 1.0
STIFFNESS = 8.0
GRAVITY = 4.0
THERMAL = 0.5
NONLINEAR = 0.4
CABBELING = 0.3
HALINE = 0.8


def extended(shard, sides, width):
    edges = {}
    for axis, dim in sides:
        size, length = (lax.axis_size(axis), shard.shape[dim])
        up = [(i, (i + 1) % size) for i in range(size)]
        last = lax.slice_in_dim(shard, length - width, length, axis=dim)
        first = lax.slice_in_dim(shard, 0, width, axis=dim)
        edges[dim] = (
            lax.ppermute(last, axis, up),
            lax.ppermute(first, axis, [(b, a) for a, b in up]),
        )
    done = []
    for _, dim in sides:
        low, high = edges[dim]
        around = [(width, width) if d in done else (0, 0) for d in range(shard.ndim)]
        shard = jnp.concatenate([jnp.pad(low, around), shard, jnp.pad(high, around)], axis=dim)
        done.append(dim)
    return shard


def over_axes(shard, axes):
    for axis in axes:
        shard = lax.psum(shard, axis)
    return shard


def shifted(value, axis, steps):
    count = lax.axis_size(axis)
    pairs = [(source, (source + steps) % count) for source in range(count)]
    return lax.ppermute(value, axis, pairs)


def from_behind(value, axis, steps):
    count = lax.axis_size(axis)
    first, last = (max(0, -steps), min(count, count - steps))
    return lax.ppermute(value, axis, [(source, source + steps) for source in range(first, last)])


def clear_walls(padded, row_axis):
    row_index = lax.broadcasted_iota(jnp.int32, padded.shape, row_axis)
    row_count = padded.shape[row_axis]
    lower_wall = (row_index == 0) & (lax.axis_index(GY) == 0)
    upper_wall = (row_index == row_count - 1) & (lax.axis_index(GY) == lax.axis_size(GY) - 1)
    return jnp.where(lower_wall | upper_wall, jnp.zeros_like(padded), padded)


def side_cells(padded):
    return (
        padded[..., 1:-1, :-2],
        padded[..., 1:-1, 2:],
        padded[..., :-2, 1:-1],
        padded[..., 2:, 1:-1],
    )


def surface_apply(grid_field, face_weights):
    padded = extended(grid_field, ((GX, 1), (GY, 0)), 1)
    applied = grid_field
    for face_weight, nearby in zip(face_weights, side_cells(padded)):
        applied = applied + face_weight * (grid_field - nearby)
    return applied


def paired(residual, image_field):
    return (
        over_axes(jnp.sum(residual * residual), GX_GY),
        over_axes(jnp.sum(residual * image_field), GX_GY),
    )


def body(
    temp_adjoint,
    height_adjoint,
    east_velocity,
    north_velocity,
    temp_store,
    salt_store,
    slot_map,
    land_mask,
    ocean_depth,
):
    half_cycle = lax.axis_size(GX) // 2
    slot_order = slot_map.reshape(-1)
    both_states = jnp.take(jnp.stack((temp_store, salt_store)), slot_order, axis=1)
    fetched = shifted(both_states, GX, half_cycle)
    wet_cells = land_mask.astype(jnp.float32)
    masked = wet_cells * temp_adjoint
    east_coef = DIFFUSE - 0.5 * east_velocity
    west_coef = DIFFUSE + 0.5 * east_velocity
    north_coef = DIFFUSE - 0.5 * north_velocity
    south_coef = DIFFUSE + 0.5 * north_velocity
    east_flux = east_coef * masked
    west_flux = west_coef * masked
    north_flux = north_coef * masked
    south_flux = south_coef * masked
    from_west = shifted(east_flux[:, :, -1:], GX, 1)
    from_east = shifted(west_flux[:, :, :1], GX, -1)
    from_south = from_behind(north_flux[:, -1:, :], GY, 1)
    from_north = from_behind(south_flux[:, :1, :], GY, -1)
    inflow = jnp.concatenate([from_west, east_flux[:, :, :-1]], axis=2)
    inflow = inflow + jnp.concatenate([west_flux[:, :, 1:], from_east], axis=2)
    inflow = inflow + jnp.concatenate([from_south, north_flux[:, :-1, :]], axis=1)
    inflow = inflow + jnp.concatenate([south_flux[:, 1:, :], from_north], axis=1)
    tracer_back = masked + TIMESTEP * (
        inflow - (east_coef + west_coef + north_coef + south_coef) * masked
    )
    open_cells = wet_cells[0]
    geometry = extended(jnp.stack((open_cells, ocean_depth)), ((GX, 2), (GY, 1)), 1)
    geometry = clear_walls(geometry, 1)
    face_links = [open_cells * nearby for nearby in side_cells(geometry[0])]
    face_weights = [
        STIFFNESS * 0.5 * (ocean_depth + nearby) * link_open
        for nearby, link_open in zip(side_cells(geometry[1]), face_links)
    ]
    target = open_cells * height_adjoint
    solution = jnp.zeros_like(target)
    residual = target
    image_field = surface_apply(residual, face_weights)
    norm_now, product = paired(residual, image_field)
    step_size = norm_now / product
    direction = residual
    along_dir = image_field
    for iteration in range(ITERS):
        solution = solution + step_size * direction
        if iteration + 1 < ITERS:
            residual = residual - step_size * along_dir
            image_field = surface_apply(residual, face_weights)
            norm_next, product = paired(residual, image_field)
            growth = norm_next / norm_now
            step_size = norm_next / (product - growth * norm_next / step_size)
            direction = residual + growth * direction
            along_dir = image_field + growth * along_dir
            norm_now = norm_next
    height_load = ocean_depth * solution
    load_padded = extended(height_load, ((GX, 1), (GY, 0)), 1)
    pressure_pull = jnp.zeros_like(height_load)
    for link_open, nearby in zip(face_links, side_cells(load_padded)):
        pressure_pull = pressure_pull + link_open * (nearby - height_load)
    adj_pressure = -GRAVITY * pressure_pull
    levels = temp_adjoint.shape[0]
    thickness = 1.0 + jnp.arange(levels, dtype=jnp.float32) / levels
    adj_density = thickness[:, None, None] * adj_pressure[None] * wet_cells
    ck_temp = fetched[0]
    ck_salt = fetched[1]
    temp_back = (
        tracer_back + (THERMAL + 2.0 * NONLINEAR * ck_temp + CABBELING * ck_salt) * adj_density
    )
    salt_back = (HALINE + CABBELING * ck_temp) * adj_density
    return (temp_back, salt_back, solution)


def solution(mesh):
    finer = Mesh(mesh.devices.reshape(2, 8, 2, 2, 4), ("gx_0", "gx_1", "gx_2", "gy_0", "gy_1"))
    placed = (
        P(None, GY, GX),
        P(GY, GX),
        P(None, GY, GX),
        P(None, GY, GX),
        P(None, GY, GX),
        P(None, GY, GX),
        P(GX, GY, None),
        P(None, GY, GX),
        P(GY, GX),
    )
    return jax.shard_map(
        body,
        mesh=finer,
        in_specs=placed,
        out_specs=(P(None, GY, GX), P(None, GY, GX), P(GY, GX)),
        check_vma=False,
    )
```

profile of v0, /device:TPU:1, one launch (start us, length us, event | category | flops | bytes accessed | tf_op | source)
XLA Modules:
  0.0 398.8 jit_solution(4032281640166941869)
XLA Ops:
  1.9 2.2 collective-permute-start.11
  4.1 1.4 collective-permute-start.5
  5.5 3.8 collective-permute-start.8
  9.4 3.1 collective-permute-start.6
  14.2 1.4 collective-permute-start.9
  15.5 3.4 collective-permute-start.10
  20.8 4.4 %all-reduce.45 = (f32[]{:T(128)}, f32[]{:T(128)}) all-reduce(f32[]{:T(128)} %get-tuple-element.14, f32[]{:T(128)} %get-tuple-element.13), channel_id=1, replica_groups=mesh['gx_0'=2,'gx_1'=8,'gx_2'=2,'gy_0'=2,'gy_1'=4] {'gx_0'}, use_global_device_ids=true, to_apply=%region_1.2 | all-reduce | flops 2 | bytes 16 | tf_op jit(solution)/shard_map/psum | solution.py:45
  25.2 17.7 %all-reduce.21 = (f32[]{:T(128)}, f32[]{:T(128)}) all-reduce(f32[]{:T(128)} %get-tuple-element.73, f32[]{:T(128)} %get-tuple-element.74), channel_id=1, replica_groups=mesh['gx_0'=2,'gx_1'=8,'gx_2'=2,'gy_0'=2,'gy_1'=4] {'gx_1'}, use_global_device_ids=true, to_apply=%region_2.3 | all-reduce | flops 2 | bytes 16 | tf_op jit(solution)/shard_map/psum | solution.py:45
  42.8 4.7 %all-reduce.39 = (f32[]{:T(128)}, f32[]{:T(128)}) all-reduce(f32[]{:T(128)} %get-tuple-element.25, f32[]{:T(128)} %get-tuple-element.26), channel_id=1, replica_groups=mesh['gx_0'=2,'gx_1'=8,'gx_2'=2,'gy_0'=2,'gy_1'=4] {'gx_2'}, use_global_device_ids=true, to_apply=%region_3.4 | all-reduce | flops 2 | bytes 16 | tf_op jit(solution)/shard_map/psum | solution.py:45
  47.6 5.9 %all-reduce.33 = (f32[]{:T(128)}, f32[]{:T(128)}) all-reduce(f32[]{:T(128)} %get-tuple-element.61, f32[]{:T(128)} %get-tuple-element.62), channel_id=1, replica_groups=mesh['gx_0'=2,'gx_1'=8,'gx_2'=2,'gy_0'=2,'gy_1'=4] {'gy_0'}, use_global_device_ids=true, to_apply=%region_4.5 | all-reduce | flops 2 | bytes 16 | tf_op jit(solution)/shard_map/psum | solution.py:45
  53.5 10.3 %all-reduce.27 = (f32[]{:T(128)}, f32[]{:T(128)}) all-reduce(f32[]{:T(128)} %get-tuple-element.49, f32[]{:T(128)} %get-tuple-element.50), channel_id=1, replica_groups=mesh['gx_0'=2,'gx_1'=8,'gx_2'=2,'gy_0'=2,'gy_1'=4] {'gy_1'}, use_global_device_ids=true, to_apply=%region_5.6 | all-reduce | flops 2 | bytes 16 | tf_op jit(solution)/shard_map/psum | solution.py:45
  65.3 5.1 %collective-permute-start.16 = (f32[1,128]{1,0:T(1,128)S(1)}, f32[1,128]{1,0:T(1,128)S(1)}, u32[]{:S(2)}, u32[]{:S(2)}) collective-permute-start(f32[1,128]{1,0:T(1,128)S(1)} %get-tuple-element.122), channel_id=1, source_target_pairs={{1,0},{2,1},{3,2},{4,3},{5,4},{6,5},{7,6},{0,7},{9,8},{10,9},{11,1... | collective-permute-start | bytes 1544 | tf_op jit(solution)/shard_map/ppermute | solution.py:32
  70.3 3.4 collective-permute-start.13
  75.2 2.3 collective-permute-done.14
  78.3 4.5 %all-reduce.44 = (f32[]{:T(128)}, f32[]{:T(128)}) all-reduce(f32[]{:T(128)} %get-tuple-element.12, f32[]{:T(128)} %get-tuple-element.11), channel_id=1, replica_groups=mesh['gx_0'=2,'gx_1'=8,'gx_2'=2,'gy_0'=2,'gy_1'=4] {'gx_0'}, use_global_device_ids=true, to_apply=%region_13.14 | all-reduce | flops 2 | bytes 16 | tf_op jit(solution)/shard_map/psum | solution.py:45
  82.8 16.7 %all-reduce.20 = (f32[]{:T(128)}, f32[]{:T(128)}) all-reduce(f32[]{:T(128)} %get-tuple-element.71, f32[]{:T(128)} %get-tuple-element.72), channel_id=1, replica_groups=mesh['gx_0'=2,'gx_1'=8,'gx_2'=2,'gy_0'=2,'gy_1'=4] {'gx_1'}, use_global_device_ids=true, to_apply=%region_14.15 | all-reduce | flops 2 | bytes 16 | tf_op jit(solution)/shard_map/psum | solution.py:45
  99.5 4.8 %all-reduce.38 = (f32[]{:T(128)}, f32[]{:T(128)}) all-reduce(f32[]{:T(128)} %get-tuple-element.23, f32[]{:T(128)} %get-tuple-element.24), channel_id=1, replica_groups=mesh['gx_0'=2,'gx_1'=8,'gx_2'=2,'gy_0'=2,'gy_1'=4] {'gx_2'}, use_global_device_ids=true, to_apply=%region_15.16 | all-reduce | flops 2 | bytes 16 | tf_op jit(solution)/shard_map/psum | solution.py:45
  104.3 6.0 %all-reduce.32 = (f32[]{:T(128)}, f32[]{:T(128)}) all-reduce(f32[]{:T(128)} %get-tuple-element.59, f32[]{:T(128)} %get-tuple-element.60), channel_id=1, replica_groups=mesh['gx_0'=2,'gx_1'=8,'gx_2'=2,'gy_0'=2,'gy_1'=4] {'gy_0'}, use_global_device_ids=true, to_apply=%region_16.17 | all-reduce | flops 2 | bytes 16 | tf_op jit(solution)/shard_map/psum | solution.py:45
  110.3 7.0 %all-reduce.26 = (f32[]{:T(128)}, f32[]{:T(128)}) all-reduce(f32[]{:T(128)} %get-tuple-element.47, f32[]{:T(128)} %get-tuple-element.48), channel_id=1, replica_groups=mesh['gx_0'=2,'gx_1'=8,'gx_2'=2,'gy_0'=2,'gy_1'=4] {'gy_1'}, use_global_device_ids=true, to_apply=%region_17.18 | all-reduce | flops 2 | bytes 16 | tf_op jit(solution)/shard_map/psum | solution.py:45
  122.0 1.4 collective-permute-start.19
  123.3 4.0 collective-permute-start.20
  127.3 5.1 %collective-permute-start.17 = (f32[128,1]{1,0:T(8,128)S(1)}, f32[128,1]{1,0:T(8,128)S(1)}, u32[]{:S(2)}, u32[]{:S(2)}) collective-permute-start(f32[128,1]{1,0:T(8,128)S(1)} %get-tuple-element.119), channel_id=1, source_target_pairs={{0,8},{8,16},{16,24},{24,32},{32,40},{40,48},{48,56},{56,64},{64,7... | collective-permute-start | bytes 1544 | tf_op jit(solution)/shard_map/ppermute | solution.py:31
  133.9 2.4 collective-permute-done.18
  137.1 19.7 %all-reduce.43 = (f32[]{:T(128)}, f32[]{:T(128)}) all-reduce(f32[]{:T(128)} %get-tuple-element.10, f32[]{:T(128)} %get-tuple-element.9), channel_id=1, replica_groups=mesh['gx_0'=2,'gx_1'=8,'gx_2'=2,'gy_0'=2,'gy_1'=4] {'gx_0'}, use_global_device_ids=true, to_apply=%region_25.26 | all-reduce | flops 2 | bytes 16 | tf_op jit(solution)/shard_map/psum | solution.py:45
  156.8 16.2 %all-reduce.19 = (f32[]{:T(128)}, f32[]{:T(128)}) all-reduce(f32[]{:T(128)} %get-tuple-element.69, f32[]{:T(128)} %get-tuple-element.70), channel_id=1, replica_groups=mesh['gx_0'=2,'gx_1'=8,'gx_2'=2,'gy_0'=2,'gy_1'=4] {'gx_1'}, use_global_device_ids=true, to_apply=%region_26.27 | all-reduce | flops 2 | bytes 16 | tf_op jit(solution)/shard_map/psum | solution.py:45
  173.1 7.2 %all-reduce.37 = (f32[]{:T(128)}, f32[]{:T(128)}) all-reduce(f32[]{:T(128)} %get-tuple-element.21, f32[]{:T(128)} %get-tuple-element.22), channel_id=1, replica_groups=mesh['gx_0'=2,'gx_1'=8,'gx_2'=2,'gy_0'=2,'gy_1'=4] {'gx_2'}, use_global_device_ids=true, to_apply=%region_27.28 | all-reduce | flops 2 | bytes 16 | tf_op jit(solution)/shard_map/psum | solution.py:45
  180.2 5.9 %all-reduce.31 = (f32[]{:T(128)}, f32[]{:T(128)}) all-reduce(f32[]{:T(128)} %get-tuple-element.57, f32[]{:T(128)} %get-tuple-element.58), channel_id=1, replica_groups=mesh['gx_0'=2,'gx_1'=8,'gx_2'=2,'gy_0'=2,'gy_1'=4] {'gy_0'}, use_global_device_ids=true, to_apply=%region_28.29 | all-reduce | flops 2 | bytes 16 | tf_op jit(solution)/shard_map/psum | solution.py:45
  186.2 6.6 %all-reduce.25 = (f32[]{:T(128)}, f32[]{:T(128)}) all-reduce(f32[]{:T(128)} %get-tuple-element.45, f32[]{:T(128)} %get-tuple-element.46), channel_id=1, replica_groups=mesh['gx_0'=2,'gx_1'=8,'gx_2'=2,'gy_0'=2,'gy_1'=4] {'gy_1'}, use_global_device_ids=true, to_apply=%region_29.30 | all-reduce | flops 2 | bytes 16 | tf_op jit(solution)/shard_map/psum | solution.py:45
  196.7 1.5 collective-permute-start.23
  198.2 3.6 collective-permute-start.24
  201.8 3.0 collective-permute-start.21
  206.9 1.6 collective-permute-done.22
  209.3 4.4 %all-reduce.42 = (f32[]{:T(128)}, f32[]{:T(128)}) all-reduce(f32[]{:T(128)} %get-tuple-element.8, f32[]{:T(128)} %get-tuple-element.7), channel_id=1, replica_groups=mesh['gx_0'=2,'gx_1'=8,'gx_2'=2,'gy_0'=2,'gy_1'=4] {'gx_0'}, use_global_device_ids=true, to_apply=%region_37.38 | all-reduce | flops 2 | bytes 16 | tf_op jit(solution)/shard_map/psum | solution.py:45
  213.7 17.6 %all-reduce.18 = (f32[]{:T(128)}, f32[]{:T(128)}) all-reduce(f32[]{:T(128)} %get-tuple-element.67, f32[]{:T(128)} %get-tuple-element.68), channel_id=1, replica_groups=mesh['gx_0'=2,'gx_1'=8,'gx_2'=2,'gy_0'=2,'gy_1'=4] {'gx_1'}, use_global_device_ids=true, to_apply=%region_38.39 | all-reduce | flops 2 | bytes 16 | tf_op jit(solution)/shard_map/psum | solution.py:45
  231.3 4.1 %all-reduce.36 = (f32[]{:T(128)}, f32[]{:T(128)}) all-reduce(f32[]{:T(128)} %get-tuple-element.19, f32[]{:T(128)} %get-tuple-element.20), channel_id=1, replica_groups=mesh['gx_0'=2,'gx_1'=8,'gx_2'=2,'gy_0'=2,'gy_1'=4] {'gx_2'}, use_global_device_ids=true, to_apply=%region_39.40 | all-reduce | flops 2 | bytes 16 | tf_op jit(solution)/shard_map/psum | solution.py:45
  235.3 5.9 %all-reduce.30 = (f32[]{:T(128)}, f32[]{:T(128)}) all-reduce(f32[]{:T(128)} %get-tuple-element.55, f32[]{:T(128)} %get-tuple-element.56), channel_id=1, replica_groups=mesh['gx_0'=2,'gx_1'=8,'gx_2'=2,'gy_0'=2,'gy_1'=4] {'gy_0'}, use_global_device_ids=true, to_apply=%region_40.41 | all-reduce | flops 2 | bytes 16 | tf_op jit(solution)/shard_map/psum | solution.py:45
  241.3 6.9 %all-reduce.24 = (f32[]{:T(128)}, f32[]{:T(128)}) all-reduce(f32[]{:T(128)} %get-tuple-element.43, f32[]{:T(128)} %get-tuple-element.44), channel_id=1, replica_groups=mesh['gx_0'=2,'gx_1'=8,'gx_2'=2,'gy_0'=2,'gy_1'=4] {'gy_1'}, use_global_device_ids=true, to_apply=%region_41.42 | all-reduce | flops 2 | bytes 16 | tf_op jit(solution)/shard_map/psum | solution.py:45
  253.1 3.9 collective-permute-start.28
  257.1 5.7 %collective-permute-start.25 = (f32[128,1]{1,0:T(8,128)S(1)}, f32[128,1]{1,0:T(8,128)S(1)}, u32[]{:S(2)}, u32[]{:S(2)}) collective-permute-start(f32[128,1]{1,0:T(8,128)S(1)} %get-tuple-element.111), channel_id=1, source_target_pairs={{0,8},{8,16},{16,24},{24,32},{32,40},{40,48},{48,56},{56,64},{64,7... | collective-permute-start | bytes 1544 | tf_op jit(solution)/shard_map/ppermute | solution.py:31
  262.7 2.3 add_multiply_fusion.1
  265.0 1.5 collective-permute-done.26
  266.5 1.4 multiply_reduce_fusion.1
  267.9 4.5 %all-reduce.41 = (f32[]{:T(128)}, f32[]{:T(128)}) all-reduce(f32[]{:T(128)} %get-tuple-element.6, f32[]{:T(128)} %get-tuple-element.5), channel_id=1, replica_groups=mesh['gx_0'=2,'gx_1'=8,'gx_2'=2,'gy_0'=2,'gy_1'=4] {'gx_0'}, use_global_device_ids=true, to_apply=%region_49.50 | all-reduce | flops 2 | bytes 16 | tf_op jit(solution)/shard_map/psum | solution.py:45
  272.4 14.7 %all-reduce.17 = (f32[]{:T(128)}, f32[]{:T(128)}) all-reduce(f32[]{:T(128)} %get-tuple-element.65, f32[]{:T(128)} %get-tuple-element.66), channel_id=1, replica_groups=mesh['gx_0'=2,'gx_1'=8,'gx_2'=2,'gy_0'=2,'gy_1'=4] {'gx_1'}, use_global_device_ids=true, to_apply=%region_50.51 | all-reduce | flops 2 | bytes 16 | tf_op jit(solution)/shard_map/psum | solution.py:45
  287.1 4.8 %all-reduce.35 = (f32[]{:T(128)}, f32[]{:T(128)}) all-reduce(f32[]{:T(128)} %get-tuple-element.17, f32[]{:T(128)} %get-tuple-element.18), channel_id=1, replica_groups=mesh['gx_0'=2,'gx_1'=8,'gx_2'=2,'gy_0'=2,'gy_1'=4] {'gx_2'}, use_global_device_ids=true, to_apply=%region_51.52 | all-reduce | flops 2 | bytes 16 | tf_op jit(solution)/shard_map/psum | solution.py:45
  291.9 5.9 %all-reduce.29 = (f32[]{:T(128)}, f32[]{:T(128)}) all-reduce(f32[]{:T(128)} %get-tuple-element.53, f32[]{:T(128)} %get-tuple-element.54), channel_id=1, replica_groups=mesh['gx_0'=2,'gx_1'=8,'gx_2'=2,'gy_0'=2,'gy_1'=4] {'gy_0'}, use_global_device_ids=true, to_apply=%region_52.53 | all-reduce | flops 2 | bytes 16 | tf_op jit(solution)/shard_map/psum | solution.py:45
  297.8 8.1 %all-reduce.23 = (f32[]{:T(128)}, f32[]{:T(128)}) all-reduce(f32[]{:T(128)} %get-tuple-element.41, f32[]{:T(128)} %get-tuple-element.42), channel_id=1, replica_groups=mesh['gx_0'=2,'gx_1'=8,'gx_2'=2,'gy_0'=2,'gy_1'=4] {'gy_1'}, use_global_device_ids=true, to_apply=%region_53.54 | all-reduce | flops 2 | bytes 16 | tf_op jit(solution)/shard_map/psum | solution.py:45
  311.0 5.0 %collective-permute-start.32 = (f32[1,128]{1,0:T(1,128)S(1)}, f32[1,128]{1,0:T(1,128)S(1)}, u32[]{:S(2)}, u32[]{:S(2)}) collective-permute-start(f32[1,128]{1,0:T(1,128)S(1)} %get-tuple-element.106), channel_id=1, source_target_pairs={{1,0},{2,1},{3,2},{4,3},{5,4},{6,5},{7,6},{0,7},{9,8},{10,9},{11,1... | collective-permute-start | bytes 1544 | tf_op jit(solution)/shard_map/ppermute | solution.py:32
  316.0 4.0 %collective-permute-start.29 = (f32[128,1]{1,0:T(8,128)S(1)}, f32[128,1]{1,0:T(8,128)S(1)}, u32[]{:S(2)}, u32[]{:S(2)}) collective-permute-start(f32[128,1]{1,0:T(8,128)S(1)} %get-tuple-element.107), channel_id=1, source_target_pairs={{0,8},{8,16},{16,24},{24,32},{32,40},{40,48},{48,56},{56,64},{64,7... | collective-permute-start | bytes 1544 | tf_op jit(solution)/shard_map/ppermute | solution.py:31
  322.1 1.5 collective-permute-done.30
  324.5 4.5 %all-reduce.40 = (f32[]{:T(128)}, f32[]{:T(128)}) all-reduce(f32[]{:T(128)} %get-tuple-element.4, f32[]{:T(128)} %get-tuple-element.3), channel_id=1, replica_groups=mesh['gx_0'=2,'gx_1'=8,'gx_2'=2,'gy_0'=2,'gy_1'=4] {'gx_0'}, use_global_device_ids=true, to_apply=%region_61.62 | all-reduce | flops 2 | bytes 16 | tf_op jit(solution)/shard_map/psum | solution.py:45
  328.9 16.3 %all-reduce.16 = (f32[]{:T(128)}, f32[]{:T(128)}) all-reduce(f32[]{:T(128)} %get-tuple-element.63, f32[]{:T(128)} %get-tuple-element.64), channel_id=1, replica_groups=mesh['gx_0'=2,'gx_1'=8,'gx_2'=2,'gy_0'=2,'gy_1'=4] {'gx_1'}, use_global_device_ids=true, to_apply=%region_62.63 | all-reduce | flops 2 | bytes 16 | tf_op jit(solution)/shard_map/psum | solution.py:45
  345.2 4.8 %all-reduce.34 = (f32[]{:T(128)}, f32[]{:T(128)}) all-reduce(f32[]{:T(128)} %get-tuple-element.15, f32[]{:T(128)} %get-tuple-element.16), channel_id=1, replica_groups=mesh['gx_0'=2,'gx_1'=8,'gx_2'=2,'gy_0'=2,'gy_1'=4] {'gx_2'}, use_global_device_ids=true, to_apply=%region_63.64 | all-reduce | flops 2 | bytes 16 | tf_op jit(solution)/shard_map/psum | solution.py:45
  350.0 5.9 %all-reduce.28 = (f32[]{:T(128)}, f32[]{:T(128)}) all-reduce(f32[]{:T(128)} %get-tuple-element.51, f32[]{:T(128)} %get-tuple-element.52), channel_id=1, replica_groups=mesh['gx_0'=2,'gx_1'=8,'gx_2'=2,'gy_0'=2,'gy_1'=4] {'gy_0'}, use_global_device_ids=true, to_apply=%region_64.65 | all-reduce | flops 2 | bytes 16 | tf_op jit(solution)/shard_map/psum | solution.py:45
  355.9 6.7 %all-reduce.22 = (f32[]{:T(128)}, f32[]{:T(128)}) all-reduce(f32[]{:T(128)} %get-tuple-element.39, f32[]{:T(128)} %get-tuple-element.40), channel_id=1, replica_groups=mesh['gx_0'=2,'gx_1'=8,'gx_2'=2,'gy_0'=2,'gy_1'=4] {'gy_1'}, use_global_device_ids=true, to_apply=%region_65.66 | all-reduce | flops 2 | bytes 16 | tf_op jit(solution)/shard_map/psum | solution.py:45
  367.4 1.4 collective-permute-start.35
  368.9 3.7 collective-permute-start.36
  372.6 5.5 %collective-permute-start.33 = (f32[128,1]{1,0:T(8,128)S(1)}, f32[128,1]{1,0:T(8,128)S(1)}, u32[]{:S(2)}, u32[]{:S(2)}) collective-permute-start(f32[128,1]{1,0:T(8,128)S(1)} %get-tuple-element.103), channel_id=1, source_target_pairs={{0,8},{8,16},{16,24},{24,32},{32,40},{40,48},{48,56},{56,64},{64,7... | collective-permute-start | bytes 1544 | tf_op jit(solution)/shard_map/ppermute | solution.py:31
  378.5 1.4 collective-permute-start.3
  380.0 4.0 collective-permute-start.2
  384.0 2.4 collective-permute-start
  388.1 4.3 %collective-permute-done = f32[8,128,1]{2,1,0:T(8,128)S(1)} collective-permute-done((f32[8,128,1]{2,1,0:T(8,128)S(1)}, f32[8,128,1]{2,1,0:T(8,128)S(1)}, u32[]{:S(2)}, u32[]{:S(2)}) %collective-permute-start) | collective-permute-done | bytes 4128 | tf_op jit(solution)/shard_map/ppermute | solution.py:52
  392.5 2.8 collective-permute-done.1
  395.8 2.9 bitcast_multiply_fusion
  (118 shorter events, 21.4 us)
Async XLA Ops:
  0.6 1.2 copy-start.11
  0.6 12.6 %copy-start.10 = (f32[8,128,128]{2,1,0:T(8,128)S(1)}, f32[8,128,128]{2,1,0:T(8,128)}, u32[]{:S(2)}) copy-start(f32[8,128,128]{2,1,0:T(8,128)} %param.13) | copy-start | bytes 1572868
  1.8 18.1 %copy-start.7 = (f32[8,128,128]{2,1,0:T(8,128)}, f32[8,128,128]{2,1,0:T(8,128)S(1)}, u32[]{:S(2)}) copy-start(f32[8,128,128]{2,1,0:T(8,128)S(1)} %convert_element_type.21) | copy-start | bytes 1572868
  1.9 2.2 copy-start.6
  1.9 11.4 %copy-start.9 = (f32[8,128,128]{2,1,0:T(8,128)S(1)}, f32[8,128,128]{2,1,0:T(8,128)}, u32[]{:S(2)}) copy-start(f32[8,128,128]{2,1,0:T(8,128)} %param.14) | copy-start | bytes 1572868
  1.9 17.4 %collective-permute-start.11 = (f32[1,128]{1,0:T(1,128)S(1)}, f32[1,128]{1,0:T(1,128)S(1)}, u32[]{:S(2)}, u32[]{:S(2)}) collective-permute-start(f32[1,128]{1,0:T(1,128)S(1)} %get-tuple-element.125), channel_id=1, source_target_pairs={{0,1},{1,2},{2,3},{3,4},{4,5},{5,6},{6,7},{7,0},{8,9},{9,10},{10,1... | collective-permute-start | bytes 1544 | tf_op jit(solution)/shard_map/ppermute | solution.py:31
  4.1 9.3 %collective-permute-start.5 = (f32[2,1,128]{2,1,0:T(1,128)S(1)}, f32[2,1,128]{2,1,0:T(1,128)S(1)}, u32[]{:S(2)}, u32[]{:S(2)}) collective-permute-start(f32[2,1,128]{2,1,0:T(1,128)S(1)} %get-tuple-element.99), channel_id=1, source_target_pairs={{0,1},{1,2},{2,3},{3,4},{4,5},{5,6},{6,7},{7,0},{8,9},{9,10},{10,1... | collective-permute-start | bytes 3080 | tf_op jit(solution)/shard_map/ppermute | solution.py:31
  5.5 8.7 %collective-permute-start.8 = (f32[2,1,128]{2,1,0:T(1,128)S(1)}, f32[2,1,128]{2,1,0:T(1,128)S(1)}, u32[]{:S(2)}, u32[]{:S(2)}) collective-permute-start(f32[2,1,128]{2,1,0:T(1,128)S(1)} %get-tuple-element.100), channel_id=1, source_target_pairs={{1,0},{2,1},{3,2},{4,3},{5,4},{6,5},{7,6},{0,7},{9,8},{10,9},{11,1... | collective-permute-start | bytes 3080 | tf_op jit(solution)/shard_map/ppermute | solution.py:32
  9.4 6.2 %collective-permute-start.6 = (f32[2,128,1]{2,1,0:T(8,128)S(1)}, f32[2,128,1]{2,1,0:T(8,128)S(1)}, u32[]{:S(2)}, u32[]{:S(2)}) collective-permute-start(f32[2,128,1]{2,1,0:T(8,128)S(1)} %get-tuple-element.97), channel_id=1, source_target_pairs={{0,8},{8,16},{16,24},{24,32},{32,40},{40,48},{48,56},{56,64},{64,7... | collective-permute-start | bytes 3080 | tf_op jit(solution)/shard_map/ppermute | solution.py:31
  12.5 0.7 copy-start.13
  12.5 6.5 %collective-permute-start.7 = (f32[2,128,1]{2,1,0:T(8,128)S(1)}, f32[2,128,1]{2,1,0:T(8,128)S(1)}, u32[]{:S(2)}, u32[]{:S(2)}) collective-permute-start(f32[2,128,1]{2,1,0:T(8,128)S(1)} %get-tuple-element.98), channel_id=1, source_target_pairs={{8,0},{16,8},{24,16},{32,24},{40,32},{48,40},{56,48},{64,56},{72,6... | collective-permute-start | bytes 3080 | tf_op jit(solution)/shard_map/ppermute | solution.py:32
  13.4 5.9 %collective-permute-start.12 = (f32[1,128]{1,0:T(1,128)S(1)}, f32[1,128]{1,0:T(1,128)S(1)}, u32[]{:S(2)}, u32[]{:S(2)}) collective-permute-start(f32[1,128]{1,0:T(1,128)S(1)} %get-tuple-element.126), channel_id=1, source_target_pairs={{1,0},{2,1},{3,2},{4,3},{5,4},{6,5},{7,6},{0,7},{9,8},{10,9},{11,1... | collective-permute-start | bytes 1544 | tf_op jit(solution)/shard_map/ppermute | solution.py:32
  14.2 5.1 %collective-permute-start.9 = (f32[128,1]{1,0:T(8,128)S(1)}, f32[128,1]{1,0:T(8,128)S(1)}, u32[]{:S(2)}, u32[]{:S(2)}) collective-permute-start(f32[128,1]{1,0:T(8,128)S(1)} %get-tuple-element.127), channel_id=1, source_target_pairs={{0,8},{8,16},{16,24},{24,32},{32,40},{40,48},{48,56},{56,64},{64,7... | collective-permute-start | bytes 1544 | tf_op jit(solution)/shard_map/ppermute | solution.py:31
  15.5 4.3 %collective-permute-start.10 = (f32[128,1]{1,0:T(8,128)S(1)}, f32[128,1]{1,0:T(8,128)S(1)}, u32[]{:S(2)}, u32[]{:S(2)}) collective-permute-start(f32[128,1]{1,0:T(8,128)S(1)} %get-tuple-element.128), channel_id=1, source_target_pairs={{8,0},{16,8},{24,16},{32,24},{40,32},{48,40},{56,48},{64,56},{72,6... | collective-permute-start | bytes 1544 | tf_op jit(solution)/shard_map/ppermute | solution.py:32
  65.2 9.8 %collective-permute-start.15 = (f32[1,128]{1,0:T(1,128)S(1)}, f32[1,128]{1,0:T(1,128)S(1)}, u32[]{:S(2)}, u32[]{:S(2)}) collective-permute-start(f32[1,128]{1,0:T(1,128)S(1)} %get-tuple-element.121), channel_id=1, source_target_pairs={{0,1},{1,2},{2,3},{3,4},{4,5},{5,6},{6,7},{7,0},{8,9},{9,10},{10,1... | collective-permute-start | bytes 1544 | tf_op jit(solution)/shard_map/ppermute | solution.py:31
  65.3 9.8 %collective-permute-start.16 = (f32[1,128]{1,0:T(1,128)S(1)}, f32[1,128]{1,0:T(1,128)S(1)}, u32[]{:S(2)}, u32[]{:S(2)}) collective-permute-start(f32[1,128]{1,0:T(1,128)S(1)} %get-tuple-element.122), channel_id=1, source_target_pairs={{1,0},{2,1},{3,2},{4,3},{5,4},{6,5},{7,6},{0,7},{9,8},{10,9},{11,1... | collective-permute-start | bytes 1544 | tf_op jit(solution)/shard_map/ppermute | solution.py:32
  70.3 4.8 %collective-permute-start.13 = (f32[128,1]{1,0:T(8,128)S(1)}, f32[128,1]{1,0:T(8,128)S(1)}, u32[]{:S(2)}, u32[]{:S(2)}) collective-permute-start(f32[128,1]{1,0:T(8,128)S(1)} %get-tuple-element.123), channel_id=1, source_target_pairs={{0,8},{8,16},{16,24},{24,32},{32,40},{40,48},{48,56},{56,64},{64,7... | collective-permute-start | bytes 1544 | tf_op jit(solution)/shard_map/ppermute | solution.py:31
  73.8 3.7 collective-permute-start.14
  122.0 11.9 %collective-permute-start.19 = (f32[1,128]{1,0:T(1,128)S(1)}, f32[1,128]{1,0:T(1,128)S(1)}, u32[]{:S(2)}, u32[]{:S(2)}) collective-permute-start(f32[1,128]{1,0:T(1,128)S(1)} %get-tuple-element.117), channel_id=1, source_target_pairs={{0,1},{1,2},{2,3},{3,4},{4,5},{5,6},{6,7},{7,0},{8,9},{9,10},{10,1... | collective-permute-start | bytes 1544 | tf_op jit(solution)/shard_map/ppermute | solution.py:31
  123.3 10.6 %collective-permute-start.20 = (f32[1,128]{1,0:T(1,128)S(1)}, f32[1,128]{1,0:T(1,128)S(1)}, u32[]{:S(2)}, u32[]{:S(2)}) collective-permute-start(f32[1,128]{1,0:T(1,128)S(1)} %get-tuple-element.118), channel_id=1, source_target_pairs={{1,0},{2,1},{3,2},{4,3},{5,4},{6,5},{7,6},{0,7},{9,8},{10,9},{11,1... | collective-permute-start | bytes 1544 | tf_op jit(solution)/shard_map/ppermute | solution.py:32
  127.3 6.6 %collective-permute-start.17 = (f32[128,1]{1,0:T(8,128)S(1)}, f32[128,1]{1,0:T(8,128)S(1)}, u32[]{:S(2)}, u32[]{:S(2)}) collective-permute-start(f32[128,1]{1,0:T(8,128)S(1)} %get-tuple-element.119), channel_id=1, source_target_pairs={{0,8},{8,16},{16,24},{24,32},{32,40},{40,48},{48,56},{56,64},{64,7... | collective-permute-start | bytes 1544 | tf_op jit(solution)/shard_map/ppermute | solution.py:31
  132.4 4.0 collective-permute-start.18
  133.6 72.1 %copy-start = (s32[8,128,128]{2,1,0:T(8,128)S(1)}, s32[8,128,128]{2,1,0:T(8,128)}, u32[]{:S(2)}) copy-start(s32[8,128,128]{2,1,0:T(8,128)} %param.16) | copy-start | bytes 1572868
  133.6 72.1 %copy-start.1 = (f32[8,128,128]{2,1,0:T(8,128)S(1)}, f32[8,128,128]{2,1,0:T(8,128)}, u32[]{:S(2)}) copy-start(f32[8,128,128]{2,1,0:T(8,128)} %param.12) | copy-start | bytes 1572868
  133.6 261.7 %collective-permute-start.4 = (f32[2,8,128,128]{3,2,0,1:T(8,128)}, f32[2,8,128,128]{3,2,0,1:T(8,128)}, u32[]{:S(2)}, u32[]{:S(2)}) collective-permute-start(f32[2,8,128,128]{3,2,0,1:T(8,128)} %select_bitcast_fusion), channel_id=1, source_target_pairs={{0,128},{8,136},{16,144},{24,152},{32,160},{40,168},{48,176},{56,1... | collective-permute-start | bytes 3145736 | tf_op jit(solution)/shard_map/ppermute | solution.py:52
  196.7 10.1 %collective-permute-start.23 = (f32[1,128]{1,0:T(1,128)S(1)}, f32[1,128]{1,0:T(1,128)S(1)}, u32[]{:S(2)}, u32[]{:S(2)}) collective-permute-start(f32[1,128]{1,0:T(1,128)S(1)} %get-tuple-element.113), channel_id=1, source_target_pairs={{0,1},{1,2},{2,3},{3,4},{4,5},{5,6},{6,7},{7,0},{8,9},{9,10},{10,1... | collective-permute-start | bytes 1544 | tf_op jit(solution)/shard_map/ppermute | solution.py:31
  198.2 8.7 %collective-permute-start.24 = (f32[1,128]{1,0:T(1,128)S(1)}, f32[1,128]{1,0:T(1,128)S(1)}, u32[]{:S(2)}, u32[]{:S(2)}) collective-permute-start(f32[1,128]{1,0:T(1,128)S(1)} %get-tuple-element.114), channel_id=1, source_target_pairs={{1,0},{2,1},{3,2},{4,3},{5,4},{6,5},{7,6},{0,7},{9,8},{10,9},{11,1... | collective-permute-start | bytes 1544 | tf_op jit(solution)/shard_map/ppermute | solution.py:32
  201.8 5.0 %collective-permute-start.21 = (f32[128,1]{1,0:T(8,128)S(1)}, f32[128,1]{1,0:T(8,128)S(1)}, u32[]{:S(2)}, u32[]{:S(2)}) collective-permute-start(f32[128,1]{1,0:T(8,128)S(1)} %get-tuple-element.115), channel_id=1, source_target_pairs={{0,8},{8,16},{16,24},{24,32},{32,40},{40,48},{48,56},{56,64},{64,7... | collective-permute-start | bytes 1544 | tf_op jit(solution)/shard_map/ppermute | solution.py:31
  204.8 3.7 collective-permute-start.22
  209.3 42.6 %copy-start.8 = (f32[128,128]{1,0:T(8,128)}, f32[128,128]{1,0:T(8,128)S(1)}, u32[]{:S(2)}) copy-start(f32[128,128]{1,0:T(8,128)S(1)} %get-tuple-element.78) | copy-start | bytes 196612
  251.9 13.1 %collective-permute-start.27 = (f32[1,128]{1,0:T(1,128)S(1)}, f32[1,128]{1,0:T(1,128)S(1)}, u32[]{:S(2)}, u32[]{:S(2)}) collective-permute-start(f32[1,128]{1,0:T(1,128)S(1)} %get-tuple-element.109), channel_id=1, source_target_pairs={{0,1},{1,2},{2,3},{3,4},{4,5},{5,6},{6,7},{7,0},{8,9},{9,10},{10,1... | collective-permute-start | bytes 1544 | tf_op jit(solution)/shard_map/ppermute | solution.py:31
  253.1 11.9 %collective-permute-start.28 = (f32[1,128]{1,0:T(1,128)S(1)}, f32[1,128]{1,0:T(1,128)S(1)}, u32[]{:S(2)}, u32[]{:S(2)}) collective-permute-start(f32[1,128]{1,0:T(1,128)S(1)} %get-tuple-element.110), channel_id=1, source_target_pairs={{1,0},{2,1},{3,2},{4,3},{5,4},{6,5},{7,6},{0,7},{9,8},{10,9},{11,1... | collective-permute-start | bytes 1544 | tf_op jit(solution)/shard_map/ppermute | solution.py:32
  257.1 8.0 %collective-permute-start.25 = (f32[128,1]{1,0:T(8,128)S(1)}, f32[128,1]{1,0:T(8,128)S(1)}, u32[]{:S(2)}, u32[]{:S(2)}) collective-permute-start(f32[128,1]{1,0:T(8,128)S(1)} %get-tuple-element.111), channel_id=1, source_target_pairs={{0,8},{8,16},{16,24},{24,32},{32,40},{40,48},{48,56},{56,64},{64,7... | collective-permute-start | bytes 1544 | tf_op jit(solution)/shard_map/ppermute | solution.py:31
  262.7 3.8 collective-permute-start.26
  310.6 11.5 %collective-permute-start.31 = (f32[1,128]{1,0:T(1,128)S(1)}, f32[1,128]{1,0:T(1,128)S(1)}, u32[]{:S(2)}, u32[]{:S(2)}) collective-permute-start(f32[1,128]{1,0:T(1,128)S(1)} %get-tuple-element.105), channel_id=1, source_target_pairs={{0,1},{1,2},{2,3},{3,4},{4,5},{5,6},{6,7},{7,0},{8,9},{9,10},{10,1... | collective-permute-start | bytes 1544 | tf_op jit(solution)/shard_map/ppermute | solution.py:31
  311.0 11.2 %collective-permute-start.32 = (f32[1,128]{1,0:T(1,128)S(1)}, f32[1,128]{1,0:T(1,128)S(1)}, u32[]{:S(2)}, u32[]{:S(2)}) collective-permute-start(f32[1,128]{1,0:T(1,128)S(1)} %get-tuple-element.106), channel_id=1, source_target_pairs={{1,0},{2,1},{3,2},{4,3},{5,4},{6,5},{7,6},{0,7},{9,8},{10,9},{11,1... | collective-permute-start | bytes 1544 | tf_op jit(solution)/shard_map/ppermute | solution.py:32
  316.0 6.2 %collective-permute-start.29 = (f32[128,1]{1,0:T(8,128)S(1)}, f32[128,1]{1,0:T(8,128)S(1)}, u32[]{:S(2)}, u32[]{:S(2)}) collective-permute-start(f32[128,1]{1,0:T(8,128)S(1)} %get-tuple-element.107), channel_id=1, source_target_pairs={{0,8},{8,16},{16,24},{24,32},{32,40},{40,48},{48,56},{56,64},{64,7... | collective-permute-start | bytes 1544 | tf_op jit(solution)/shard_map/ppermute | solution.py:31
  320.0 3.7 collective-permute-start.30
  324.4 53.6 %copy-start.5 = (f32[8,128,128]{2,1,0:T(8,128)S(1)}, f32[8,128,128]{2,1,0:T(8,128)}, u32[]{:S(2)}) copy-start(f32[8,128,128]{2,1,0:T(8,128)} %get-tuple-element.92) | copy-start | bytes 1572868
  367.4 11.2 %collective-permute-start.35 = (f32[1,128]{1,0:T(1,128)S(1)}, f32[1,128]{1,0:T(1,128)S(1)}, u32[]{:S(2)}, u32[]{:S(2)}) collective-permute-start(f32[1,128]{1,0:T(1,128)S(1)} %get-tuple-element.101), channel_id=1, source_target_pairs={{0,1},{1,2},{2,3},{3,4},{4,5},{5,6},{6,7},{7,0},{8,9},{9,10},{10,1... | collective-permute-start | bytes 1544 | tf_op jit(solution)/shard_map/ppermute | solution.py:31
  368.9 11.1 %collective-permute-start.36 = (f32[1,128]{1,0:T(1,128)S(1)}, f32[1,128]{1,0:T(1,128)S(1)}, u32[]{:S(2)}, u32[]{:S(2)}) collective-permute-start(f32[1,128]{1,0:T(1,128)S(1)} %get-tuple-element.102), channel_id=1, source_target_pairs={{1,0},{2,1},{3,2},{4,3},{5,4},{6,5},{7,6},{0,7},{9,8},{10,9},{11,1... | collective-permute-start | bytes 1544 | tf_op jit(solution)/shard_map/ppermute | solution.py:32
  372.6 11.4 %collective-permute-start.33 = (f32[128,1]{1,0:T(8,128)S(1)}, f32[128,1]{1,0:T(8,128)S(1)}, u32[]{:S(2)}, u32[]{:S(2)}) collective-permute-start(f32[128,1]{1,0:T(8,128)S(1)} %get-tuple-element.103), channel_id=1, source_target_pairs={{0,8},{8,16},{16,24},{24,32},{32,40},{40,48},{48,56},{56,64},{64,7... | collective-permute-start | bytes 1544 | tf_op jit(solution)/shard_map/ppermute | solution.py:31
  378.1 8.3 %collective-permute-start.34 = (f32[128,1]{1,0:T(8,128)S(1)}, f32[128,1]{1,0:T(8,128)S(1)}, u32[]{:S(2)}, u32[]{:S(2)}) collective-permute-start(f32[128,1]{1,0:T(8,128)S(1)} %get-tuple-element.104), channel_id=1, source_target_pairs={{8,0},{16,8},{24,16},{32,24},{40,32},{48,40},{56,48},{64,56},{72,6... | collective-permute-start | bytes 1544 | tf_op jit(solution)/shard_map/ppermute | solution.py:32
  378.3 17.0 %copy-start.3 = (f32[8,127,128]{2,1,0:T(8,128)S(1)}, f32[8,127,128]{2,1,0:T(8,128)}, u32[]{:S(2)}) copy-start(f32[8,127,128]{2,1,0:T(8,128)} %slice.360) | copy-start | bytes 1560580
  378.3 17.0 %copy-start.4 = (f32[8,128,128]{2,1,0:T(8,128)S(1)}, f32[8,128,128]{2,1,0:T(8,128)}, u32[]{:S(2)}) copy-start(f32[8,128,128]{2,1,0:T(8,128)} %param.11) | copy-start | bytes 1572868
  378.5 16.8 %copy-start.2 = (f32[8,128,128]{2,1,0:T(8,128)S(1)}, f32[8,128,128]{2,1,0:T(8,128)}, u32[]{:S(2)}) copy-start(f32[8,128,128]{2,1,0:T(8,128)} %get-tuple-element.94) | copy-start | bytes 1572868
  378.5 9.6 %collective-permute-start.3 = (f32[8,1,128]{2,1,0:T(1,128)S(1)}, f32[8,1,128]{2,1,0:T(1,128)S(1)}, u32[]{:S(2)}, u32[]{:S(2)}) collective-permute-start(f32[8,1,128]{2,1,0:T(1,128)S(1)} %slice.361), channel_id=1, source_target_pairs={{1,0},{2,1},{3,2},{4,3},{5,4},{6,5},{7,6},{9,8},{10,9},{11,10},{12... | collective-permute-start | bytes 12296 | tf_op jit(solution)/shard_map/ppermute | solution.py:58
  380.0 8.2 %collective-permute-start.2 = (f32[8,1,128]{2,1,0:T(1,128)S(1)}, f32[8,1,128]{2,1,0:T(1,128)S(1)}, u32[]{:S(2)}, u32[]{:S(2)}) collective-permute-start(f32[8,1,128]{2,1,0:T(1,128)S(1)} %slice.358), channel_id=1, source_target_pairs={{0,1},{1,2},{2,3},{3,4},{4,5},{5,6},{6,7},{8,9},{9,10},{10,11},{11... | collective-permute-start | bytes 12296 | tf_op jit(solution)/shard_map/ppermute | solution.py:58
  384.0 8.5 %collective-permute-start = (f32[8,128,1]{2,1,0:T(8,128)S(1)}, f32[8,128,1]{2,1,0:T(8,128)S(1)}, u32[]{:S(2)}, u32[]{:S(2)}) collective-permute-start(f32[8,128,1]{2,1,0:T(8,128)S(1)} %slice.354), channel_id=1, source_target_pairs={{0,8},{8,16},{16,24},{24,32},{32,40},{40,48},{48,56},{56,64},{64,7... | collective-permute-start | bytes 12296 | tf_op jit(solution)/shard_map/ppermute | solution.py:52
  386.4 8.9 %collective-permute-start.1 = (f32[8,128,1]{2,1,0:T(8,128)S(1)}, f32[8,128,1]{2,1,0:T(8,128)S(1)}, u32[]{:S(2)}, u32[]{:S(2)}) collective-permute-start(f32[8,128,1]{2,1,0:T(8,128)S(1)} %bitcast.64), channel_id=1, source_target_pairs={{0,248},{8,0},{16,8},{24,16},{32,24},{40,32},{48,40},{56,48},{64,5... | collective-permute-start | bytes 12296 | tf_op jit(solution)/shard_map/ppermute | solution.py:52
  395.3 0.6 copy-start.12
where the time goes:
time: 401 us; the launch traced here: 399 us
  blocking collectives  253 us (63%)
  starting transfers between devices  84.3 us (21%)
  between operations  22.2 us (6%)
  other arithmetic  17.7 us (4%)
  waiting for transfers between devices  17.3 us (4%)
  local copies, waits for them, and re-layouts  4.48 us (1%)
    psum x30, blocking collectives, over_axes(): shard = lax.psum(shard, axis)  253 us
    ppermute x16, starting transfers between devices, extended(): lax.ppermute(last, axis, up)  40.7 us
    ppermute x16, starting transfers between devices, extended(): lax.ppermute(first, axis, [(b, a) for a, b in up])  34.8 us
    ppermute x16, waiting for transfers between devices, extended(): lax.ppermute(first, axis, [(b, a) for a, b in up])  10.1 us
  transfers between devices with their start and end apart: 37, of which 9 were waited for; matrix products, arithmetic and copies ran while one was open for 4% of the time, Pallas kernels for 0%

commit v1 on v0

v1 whole, which is shorter than its diff:
```python
import itertools
import functools

import jax
import jax.numpy as jnp
from jax import lax
from jax.experimental import pallas as pl
from jax.experimental.pallas import tpu as pltpu
from jax.sharding import PartitionSpec as P

DIFFUSE = 0.2
TIMESTEP = 1.0
STIFFNESS = 8.0
GRAVITY = 4.0
THERMAL = 0.5
NONLINEAR = 0.4
CABBELING = 0.3
HALINE = 0.8
ITERS = 6
SCALE = 16.0
G = 8
LEV, CY, CX = 8, 128, 128
ROWS, COLS = CY + 2 * G, 2 * CX
SIZES = {"xl": 2, "z": 8, "c": 2, "xh": 2, "y": 4}
STAGES = (("z", "c"), ("xl", "xh", "y"))
F32 = jnp.float32


def two_sum(a, b):
    s = a + b
    t = s - a
    return s, (a - (s - t)) + (b - t)


def quick(a, b):
    s = a + b
    return s, b - (s - a)


def df_add(x, y):
    s, e = two_sum(x[0], y[0])
    return quick(s, e + (x[1] + y[1]))


def df_neg(x):
    return -x[0], -x[1]


def halves(a):
    c = 4097.0 * a
    hi = c - (c - a)
    return hi, a - hi


def two_prod(a, b):
    p = a * b
    ah, al = halves(a)
    bh, bl = halves(b)
    return p, ((ah * bh - p) + ah * bl + al * bh) + al * bl


def df_mul(x, y):
    p, e = two_prod(x[0], y[0])
    return quick(p, e + (x[0] * y[1] + x[1] * y[0]))


def df_div(x, y):
    q = x[0] / y[0]
    p, e = two_prod(q, y[0])
    s, t = two_sum(x[0], -p)
    r = s + (t + (x[1] - (e + q * y[1])))
    return quick(q, r / y[0])


def peers(stage):
    return [o for o in itertools.product(*[range(SIZES[d]) for d in stage]) if any(o)]


def tree(x):
    while x.shape[0] > 8:
        h = x.shape[0] // 2
        x = x[:h] + x[h:]
    return x


def kernel(
    slot_ref, ta_h, ha_h, ev_h, nv_h, ts_h, ss_h, lm_h, od_h,
    tb_h, sb_h, sa_h,
    ta, ha, ev, nv, store, lm, od,
    stage, fetched, back, out, edge, edge_in, rows_out, rows_in, corner_in,
    zed, zed_in, zrow, zrow_in, field, depth, wgt, basis, mail, mail_in, sol,
    load_sem, bulk_sem, halo_sem, zed_sem, mail_sem, out_sem,
):
    gx, gy = lax.axis_index("gx"), lax.axis_index("gy")
    co = {"xl": gx // 16, "z": (gx // 2) % 8, "c": gx % 2, "xh": gy // 4, "y": gy % 4}

    def peer(st, off):
        n = dict(co)
        for d, o in zip(st, off):
            n[d] = (co[d] + o) % SIZES[d]
        return (n["xl"] * 16 + n["z"] * 2 + n["c"], n["xh"] * 4 + n["y"])

    west, east = (gx + 31) % 32, (gx + 1) % 32
    south, north = (gy + 7) % 8, (gy + 1) % 8
    partner = ((gx + 16) % 32, gy)

    local = [
        (od_h, od), (lm_h.at[0], lm.at[0]), (ha_h, ha),
        (ts_h, store.at[0]), (ss_h, store.at[1]),
        (lm_h.at[pl.ds(1, LEV - 1)], lm.at[pl.ds(1, LEV - 1)]),
        (ta_h, ta), (ev_h, ev), (nv_h, nv),
    ]
    loads = [pltpu.make_async_copy(a, b, load_sem.at[i]) for i, (a, b) in enumerate(local)]
    for c in loads:
        c.start()

    barrier = pltpu.get_barrier_semaphore()
    greeted = [peer(st, off) for st in STAGES for off in peers(st)]
    greeted += [(a, b) for a in (west, east) for b in (south, gy, north)]
    for who in greeted:
        pl.semaphore_signal(barrier, inc=1, device_id=who)

    lane = lax.broadcasted_iota(jnp.int32, (CY, CX), 1)
    row = lax.broadcasted_iota(jnp.int32, (CY, CX), 0)
    lane8 = lane[:8]

    for c in loads[:3]:
        c.wait()
    opened = lm[0].astype(F32)
    target = opened * ha[...]
    dm = opened * od[...]
    field[pl.ds(G, CY), pl.ds(0, CX)] = target
    depth[pl.ds(G, CY), pl.ds(0, CX)] = dm
    edge[...] = jnp.where(
        (lane < 8) | (lane >= 120),
        target,
        jnp.where(lane < 64, pltpu.roll(dm, 8, 1), pltpu.roll(dm, 120, 1)),
    )
    rows_out[0, 0] = target[:8]
    rows_out[0, 1] = dm[:8]
    rows_out[1, 0] = target[120:]
    rows_out[1, 1] = dm[120:]

    for c in loads[3:5]:
        c.wait()
    for k in range(LEV):
        slot = slot_ref[0, 0, k]
        stage[0, k] = store[0, slot]
        stage[1, k] = store[1, slot]

    pl.semaphore_wait(barrier, len(greeted))

    low, high = pl.ds(0, 8), pl.ds(120, 8)
    halo = [
        (edge, edge_in.at[0], (west, gy)),
        (edge, edge_in.at[1], (east, gy)),
        (rows_out.at[0], rows_in.at[0], (gx, south)),
        (rows_out.at[1], rows_in.at[1], (gx, north)),
        (edge.at[low], corner_in.at[0], (west, south)),
        (edge.at[low], corner_in.at[1], (east, south)),
        (edge.at[high], corner_in.at[2], (west, north)),
        (edge.at[high], corner_in.at[3], (east, north)),
    ]
    halos = []
    for i, (a, b, who) in enumerate(halo):
        c = pltpu.make_async_remote_copy(a, b, halo_sem.at[0, i], halo_sem.at[1, i], device_id=who)
        c.start()
        halos.append(c)
    bulks = []
    for k in range(LEV):
        c = pltpu.make_async_remote_copy(
            stage.at[:, k], fetched.at[:, k], bulk_sem.at[0, k], bulk_sem.at[1, k], device_id=partner
        )
        c.start()
        bulks.append(c)

    for c in halos:
        c.wait_recv()
    has_north = jnp.where(gy < 7, 1.0, 0.0).astype(F32)
    has_south = jnp.where(gy > 0, 1.0, 0.0).astype(F32)

    def side(east_tile, west_tile, lanes):
        got = jnp.where(lanes < 64, east_tile, west_tile)
        n = got.shape[0]
        inner = jnp.where(lanes < 64, pltpu.roll(got, 120, 1), pltpu.roll(got, 8, 1))
        return got, inner

    mid, top, bottom = pl.ds(G, CY), pl.ds(G + CY, G), pl.ds(0, G)
    own, far = pl.ds(0, CX), pl.ds(CX, CX)
    a, b = side(edge_in[0], edge_in[1], lane)
    field[mid, far] = a
    depth[mid, far] = b
    a, b = side(corner_in[0], corner_in[1], lane8)
    field[top, far] = a * has_north
    depth[top, far] = b * has_north
    a, b = side(corner_in[2], corner_in[3], lane8)
    field[bottom, far] = a * has_south
    depth[bottom, far] = b * has_south
    field[top, own] = rows_in[0, 0] * has_north
    depth[top, own] = rows_in[0, 1] * has_north
    field[bottom, own] = rows_in[1, 0] * has_south
    depth[bottom, own] = rows_in[1, 1] * has_south

    d = depth[...]
    for i, (shift, axis) in enumerate(((1, 1), (COLS - 1, 1), (1, 0), (ROWS - 1, 0))):
        e = pltpu.roll(d, shift, axis)
        wgt[i] = jnp.where((d > 0.0) & (e > 0.0), (STIFFNESS * 0.5 / SCALE) * (d + e), 0.0)

    def apply(v):
        return (
            wgt[0] * (v - pltpu.roll(v, 1, 1))
            + wgt[1] * (v - pltpu.roll(v, COLS - 1, 1))
            + wgt[2] * (v - pltpu.roll(v, 1, 0))
            + wgt[3] * (v - pltpu.roll(v, ROWS - 1, 0))
        )

    partial = []
    v = field[...]
    for k in range(ITERS):
        nxt = apply(v)
        if k == 0:
            basis[...] = nxt
        here, there = v[G : G + CY, :CX], nxt[G : G + CY, :CX]
        partial.append(tree(here * here))
        partial.append(tree(here * there))
        v = nxt
    nm = len(partial)
    hi = jnp.stack(partial)
    lo = jnp.zeros_like(hi)
    for s in (4, 2, 1):
        hi, lo = df_add((hi, lo), (pltpu.roll(hi, s, 1), pltpu.roll(lo, s, 1)))
    sub8 = lax.broadcasted_iota(jnp.int32, (8, CX), 0)

    def packed(x):
        done = []
        for first in (0, 8):
            t = jnp.zeros((8, CX), F32)
            for j in range(first, min(first + 8, nm)):
                t = jnp.where(sub8 == j - first, x[j], t)
            done.append(t)
        return jnp.concatenate(done, axis=0)

    hi, lo = packed(hi), packed(lo)
    for s in (64, 32, 16, 8, 4, 2, 1):
        hi, lo = df_add((hi, lo), (pltpu.roll(hi, s, 1), pltpu.roll(lo, s, 1)))
    letter = jnp.where(
        lane8 < 64,
        jnp.where(lane8 < 32, hi[:8], hi[8:]),
        jnp.where(lane8 < 96, lo[:8], lo[8:]),
    )

    def post(st):
        mail[st] = letter
        for i, off in enumerate(peers(STAGES[st])):
            pltpu.make_async_remote_copy(
                mail.at[st], mail_in.at[st, i], mail_sem.at[0, st], mail_sem.at[1, st],
                device_id=peer(STAGES[st], off),
            ).start()

    def collect(st):
        pltpu.make_async_copy(mail_in.at[st], mail_in.at[st], mail_sem.at[1, st]).wait()
        his = [mail[st]] + [mail_in[st, i] for i in range(len(peers(STAGES[st])))]
        terms = [(t, pltpu.roll(t, 64, 1)) for t in his]
        while len(terms) > 1:
            terms = [df_add(terms[i], terms[i + 1]) for i in range(0, len(terms), 2)]
        return terms[0]

    post(0)

    for c in loads[5:]:
        c.wait()
    z = jnp.zeros((CY, CX), F32)
    zn = jnp.zeros((8, CX), F32)
    zs = jnp.zeros((8, CX), F32)
    for k in range(LEV):
        m = lm[k].astype(F32) * ta[k]
        ec = DIFFUSE - 0.5 * ev[k]
        wc = DIFFUSE + 0.5 * ev[k]
        nc = DIFFUSE - 0.5 * nv[k]
        sc = DIFFUSE + 0.5 * nv[k]
        ef, wf, nf, sf = ec * m, wc * m, nc * m, sc * m
        inflow = jnp.where(lane == 0, 0.0, pltpu.roll(ef, 1, 1))
        inflow = inflow + jnp.where(lane == CX - 1, 0.0, pltpu.roll(wf, CX - 1, 1))
        inflow = inflow + jnp.where(row == 0, 0.0, pltpu.roll(nf, 1, 0))
        inflow = inflow + jnp.where(row == CY - 1, 0.0, pltpu.roll(sf, CY - 1, 0))
        back[k] = m + TIMESTEP * (inflow - (ec + wc + nc + sc) * m)
        z = jnp.where(lane == k, pltpu.roll(wf, k, 1) if k else wf, z)
        z = jnp.where(lane == 120 + k, pltpu.roll(ef, 121 + k, 1) if k < 7 else ef, z)
        zrow[1, pl.ds(k, 1)] = nf[CY - 1 :]
        zrow[0, pl.ds(k, 1)] = sf[:1]
    zed[...] = z
    zeds = []
    for i, (a, b, who) in enumerate((
        (zed, zed_in.at[0], (west, gy)),
        (zed, zed_in.at[1], (east, gy)),
        (zrow.at[0], zrow_in.at[0], (gx, south)),
        (zrow.at[1], zrow_in.at[1], (gx, north)),
    )):
        c = pltpu.make_async_remote_copy(a, b, zed_sem.at[0, i], zed_sem.at[1, i], device_id=who)
        c.start()
        zeds.append(c)

    total = collect(0)
    letter = jnp.where(lane8 < 64, total[0], pltpu.roll(total[1], 64, 1))
    post(1)

    for c in zeds:
        c.wait_recv()
    ze, zw = zed_in[0], zed_in[1]
    for k in range(LEV):
        b = back[k]
        b = b + jnp.where(lane == 0, pltpu.roll(zw, 8 - k, 1), 0.0)
        b = b + jnp.where(lane == CX - 1, pltpu.roll(ze, 127 - k, 1), 0.0)
        b = b + jnp.where(row == 0, zrow_in[1, pl.ds(k, 1)] * has_south, 0.0)
        back[k] = b + jnp.where(row == CY - 1, zrow_in[0, pl.ds(k, 1)] * has_north, 0.0)

    total = collect(1)
    cur = tuple(jnp.concatenate([t, pltpu.roll(t, 96, 1)], axis=0) for t in total)
    prev = (jnp.zeros_like(cur[0]), jnp.zeros_like(cur[0]))

    def pick(x, k):
        return x[0][k : k + 1], x[1][k : k + 1]

    def spread(x):
        return jnp.broadcast_to(x[0], cur[0].shape), jnp.broadcast_to(x[1], cur[0].shape)

    def up(x):
        return pltpu.roll(x[0], 15, 0), pltpu.roll(x[1], 15, 0)

    norm = pick(cur, 0)
    ratio = df_div(pick(cur, 1), norm)
    ja, jb = [ratio], []
    for k in range(1, ITERS):
        nxt = df_add(up(cur), df_neg(df_mul(spread(ja[-1]), cur)))
        if k > 1:
            nxt = df_add(nxt, df_neg(df_mul(spread(jb[-1]), prev)))
        fresh = pick(nxt, k)
        new_ratio = df_div(pick(nxt, k + 1), fresh)
        ja.append(df_add(new_ratio, df_neg(ratio)))
        jb.append(df_div(fresh, norm))
        norm, ratio, prev, cur = fresh, new_ratio, cur, nxt
    steps, growths = [], []
    for k in range(ITERS):
        diag = 1.0 + SCALE * (ja[k][0] + ja[k][1])
        if k:
            off = (SCALE * SCALE) * (jb[k - 1][0] + jb[k - 1][1])
            growths.append(off * steps[-1] * steps[-1])
            diag = diag - off * steps[-1]
        steps.append(1.0 / diag)
    whole = (ROWS, COLS)
    steps = [jnp.broadcast_to(x[:1, :1], whole) for x in steps]
    growths = [jnp.broadcast_to(x[:1, :1], whole) for x in growths]

    r = field[...]
    p = r
    s = jnp.zeros_like(r)
    for k in range(ITERS):
        s = s + steps[k] * p
        if k + 1 < ITERS:
            q = p + SCALE * (basis[...] if k == 0 else apply(p))
            r = r - steps[k] * q
            p = r + growths[k] * p
    load = depth[...] * s
    pull = jnp.zeros_like(load)
    for i, (shift, axis) in enumerate(((1, 1), (COLS - 1, 1), (1, 0), (ROWS - 1, 0))):
        pull = pull + jnp.where(wgt[i] > 0.0, pltpu.roll(load, shift, axis) - load, 0.0)
    sol[...] = s[G : G + CY, :CX]
    sol_copy = pltpu.make_async_copy(sol, sa_h, out_sem.at[2, 0])
    sol_copy.start()
    pressure = -GRAVITY * pull[G : G + CY, :CX]

    outs = []
    for k in range(LEV):
        bulks[k].wait_recv()
        dens = ((1.0 + k / LEV) * pressure) * lm[k].astype(F32)
        ct, cs = fetched[0, k], fetched[1, k]
        out[0, k] = back[k] + (THERMAL + 2.0 * NONLINEAR * ct + CABBELING * cs) * dens
        out[1, k] = (HALINE + CABBELING * ct) * dens
        for i, dst in enumerate((tb_h, sb_h)):
            c = pltpu.make_async_copy(out.at[i, k], dst.at[k], out_sem.at[i, k])
            c.start()
            outs.append(c)
    for c in halos + bulks + zeds:
        c.wait_send()
    for st in range(2):
        pltpu.make_async_copy(mail_in.at[st], mail_in.at[st], mail_sem.at[0, st]).wait()
    sol_copy.wait()
    for c in outs:
        c.wait()


def body(ta, ha, ev, nv, ts, ss, slots, lm, od):
    vm = lambda *shape: pltpu.VMEM(shape, F32)
    cube = (LEV, CY, CX)
    dma = lambda *shape: pltpu.SemaphoreType.DMA(shape)
    n = len(peers(STAGES[0]))
    hbm = pl.BlockSpec(memory_space=pl.ANY)
    return pl.pallas_call(
        kernel,
        out_shape=(
            jax.ShapeDtypeStruct(cube, F32),
            jax.ShapeDtypeStruct(cube, F32),
            jax.ShapeDtypeStruct((CY, CX), F32),
        ),
        in_specs=[pl.BlockSpec(memory_space=pltpu.SMEM)] + [hbm] * 8,
        out_specs=(hbm, hbm, hbm),
        scratch_shapes=[
            vm(*cube), vm(CY, CX), vm(*cube), vm(*cube), vm(2, *cube), pltpu.VMEM(cube, jnp.int32), vm(CY, CX),
            vm(2, *cube), vm(2, *cube), vm(*cube), vm(2, *cube),
            vm(CY, CX), vm(2, CY, CX), vm(2, 2, 8, CX), vm(2, 2, 8, CX), vm(4, 8, CX),
            vm(CY, CX), vm(2, CY, CX), vm(2, 8, CX), vm(2, 8, CX),
            vm(ROWS, COLS), vm(ROWS, COLS), vm(4, ROWS, COLS), vm(ROWS, COLS),
            vm(2, 8, CX), vm(2, n, 8, CX), vm(CY, CX),
            dma(9), dma(2, LEV), dma(2, 8), dma(2, 4), dma(2, 2), dma(3, LEV),
        ],
        compiler_params=pltpu.CompilerParams(
            collective_id=0, has_side_effects=True, vmem_limit_bytes=40 << 20
        ),
        cost_estimate=pl.CostEstimate(flops=20000000, bytes_accessed=5000000, transcendentals=0),
        name="adjoint",
    )(slots, ta, ha, ev, nv, ts, ss, lm, od)


def solution(mesh):
    cube, flat = P(None, "gy", "gx"), P("gy", "gx")
    return jax.shard_map(
        body,
        mesh=mesh,
        in_specs=(cube, flat, cube, cube, cube, cube, P("gx", "gy", None), cube, flat),
        out_specs=(cube, cube, flat),
        check_vma=False,
    )
```

time: 401 us -> 56.7 us (0.14)
  blocking collectives: 253 us -> 0 us
  starting transfers between devices: 84.3 us -> 0 us
  Pallas kernels: 0 us -> 44.8 us
  between operations: 22.2 us -> 0.66 us
  other arithmetic: 17.7 us -> 0 us
  waiting for transfers between devices: 17.3 us -> 0 us
  local copies, waits for them, and re-layouts: 4.48 us -> 10.8 us
    psum x30 -> x0, blocking collectives: 253 us -> none  [over_axes(): shard = lax.psum(shard, axis)]
    ppermute x37 -> x0, starting transfers between devices: 84.3 us -> none  [the longest x16 40.7 us: extended(): lax.ppermute(last, axis, up)]
    pallas_call x0 -> x1, Pallas kernels: none -> 44.8 us  [body(): pl.pallas_call(kernel, out_shape=(jax.ShapeDtypeStruct(cube, F32), jax.Sh...]
    ppermute x37 -> x0, waiting for transfers between devices: 17.3 us -> none  [the longest x16 10.1 us: extended(): lax.ppermute(first, axis, [(b, a) for a, b in up])]
    unnamed x28 -> x21, local copies, waits for them, and re-layouts: 1.25 us -> 10.8 us
    mul x6 -> x0, other arithmetic: 8.16 us -> none  [the longest x1 2.93 us: body(): salt_back = (HALINE + CABBELING * ck_temp) * adj_density]
    reduce_sum x6 -> x0, other arithmetic: 5.38 us -> none  [paired(): jnp.sum(residual * image_field)]
  transfers between devices with their start and end apart: 37 -> 0, of which waited for: 9 -> 0; matrix products, arithmetic and copies ran while one was open for 4% -> 0% of each run, Pallas kernels for 0% -> 0%
where the time goes in v1:
time: 56.7 us; the launch traced here: 56.3 us
  Pallas kernels  44.8 us (79%)
  local copies, waits for them, and re-layouts  10.8 us (19%)
  between operations  0.66 us (1%)
    pallas_call x1, Pallas kernels, body(): pl.pallas_call(kernel, out_shape=(jax.ShapeDtypeStruct(cube, F32), jax.Sh...  44.8 us
    unnamed x21, local copies, waits for them, and re-layouts  10.8 us

profile of v1, /device:TPU:1, one launch (start us, length us, event | category | flops | bytes accessed | tf_op | source)
XLA Modules:
  0.0 56.3 jit_solution(8432862442172903245)
XLA Ops:
  0.6 0.0 copy-start
  0.6 1.0 %copy-done = f32[8,128,128]{2,1,0:T(8,128)S(1)} copy-done((f32[8,128,128]{2,1,0:T(8,128)S(1)}, f32[8,128,128]{2,1,0:T(8,128)}, u32[]{:S(2)}) %copy-start) | copy-done | bytes 524312
  1.7 0.0 copy-start.1
  1.7 1.0 %copy-done.1 = f32[8,128,128]{2,1,0:T(8,128)S(1)} copy-done((f32[8,128,128]{2,1,0:T(8,128)S(1)}, f32[8,128,128]{2,1,0:T(8,128)}, u32[]{:S(2)}) %copy-start.1) | copy-done | bytes 524312
  2.7 0.0 copy-start.2
  2.7 1.0 %copy-done.2 = f32[8,128,128]{2,1,0:T(8,128)S(1)} copy-done((f32[8,128,128]{2,1,0:T(8,128)S(1)}, f32[8,128,128]{2,1,0:T(8,128)}, u32[]{:S(2)}) %copy-start.2) | copy-done | bytes 524312
  3.8 0.0 copy-start.3
  3.8 1.0 %copy-done.3 = f32[8,128,128]{2,1,0:T(8,128)S(1)} copy-done((f32[8,128,128]{2,1,0:T(8,128)S(1)}, f32[8,128,128]{2,1,0:T(8,128)}, u32[]{:S(2)}) %copy-start.3) | copy-done | bytes 524312
  4.8 0.0 copy-start.4
  4.8 1.0 %copy-done.4 = f32[8,128,128]{2,1,0:T(8,128)S(1)} copy-done((f32[8,128,128]{2,1,0:T(8,128)S(1)}, f32[8,128,128]{2,1,0:T(8,128)}, u32[]{:S(2)}) %copy-start.4) | copy-done | bytes 524312
  5.8 0.0 copy-start.5
  5.8 1.0 %copy-done.5 = s32[8,128,128]{2,1,0:T(8,128)S(1)} copy-done((s32[8,128,128]{2,1,0:T(8,128)S(1)}, s32[8,128,128]{2,1,0:T(8,128)}, u32[]{:S(2)}) %copy-start.5) | copy-done | bytes 524312
  6.9 0.0 copy-start.6
  6.9 0.8 %copy-done.6 = f32[128,128]{1,0:T(8,128)S(1)} copy-done((f32[128,128]{1,0:T(8,128)S(1)}, f32[128,128]{1,0:T(8,128)}, u32[]{:S(2)}) %copy-start.6) | copy-done | bytes 65560
  7.7 0.0 copy-start.7
  7.7 0.8 %copy-done.7 = f32[128,128]{1,0:T(8,128)S(1)} copy-done((f32[128,128]{1,0:T(8,128)S(1)}, f32[128,128]{1,0:T(8,128)}, u32[]{:S(2)}) %copy-start.7) | copy-done | bytes 65560
  8.6 0.0 copy-start.8
  8.6 0.7 %copy-done.8 = s32[1,1,8]{2,1,0:T(1,128)S(1)} copy-done((s32[1,1,8]{2,1,0:T(1,128)S(1)}, s32[1,1,8]{2,1,0:T(1,128)}, u32[]{:S(2)}) %copy-start.8) | copy-done | bytes 56
  9.2 44.8 %adjoint.1 = (f32[8,128,128]{2,1,0:T(8,128)S(1)}, f32[8,128,128]{2,1,0:T(8,128)S(1)}, f32[128,128]{1,0:T(8,128)S(1)}) custom-call(s32[1,1,8]{2,1,0:T(1,128)S(1)} %copy-done.8, f32[8,128,128]{2,1,0:T(8,128)S(1)} %copy-done, f32[128,128]{1,0:T(8,128)S(1)} %copy-done.6, f32[8,128,128]{2,1,0:T(8,128)S(1)} %copy-done.1, f32[8,128,128]{2,1,0:T(8,128)S(1)} %copy-done.2, ...), custom_call_target="tpu_custom_call" | custom-call | flops 20000000 | bytes 5000000 | tf_op jit(solution)/shard_map/adjoint/pallas_call | solution.py:398
  54.0 0.8 %copy.15 = f32[8,128,128]{2,1,0:T(8,128)} copy(f32[8,128,128]{2,1,0:T(8,128)S(1)} %get-tuple-element.6) | data formatting | bytes 1048576
  54.8 0.8 %copy.16 = f32[8,128,128]{2,1,0:T(8,128)} copy(f32[8,128,128]{2,1,0:T(8,128)S(1)} %get-tuple-element.7) | data formatting | bytes 1048576
  55.6 0.6 %copy.17 = f32[128,128]{1,0:T(8,128)} copy(f32[128,128]{1,0:T(8,128)S(1)} %get-tuple-element.8) | data formatting | bytes 131072
Async XLA Ops:
  0.6 1.0 %copy-start = (f32[8,128,128]{2,1,0:T(8,128)S(1)}, f32[8,128,128]{2,1,0:T(8,128)}, u32[]{:S(2)}) copy-start(f32[8,128,128]{2,1,0:T(8,128)} %ta_h.1) | copy-start | bytes 1572868
  1.7 1.0 %copy-start.1 = (f32[8,128,128]{2,1,0:T(8,128)S(1)}, f32[8,128,128]{2,1,0:T(8,128)}, u32[]{:S(2)}) copy-start(f32[8,128,128]{2,1,0:T(8,128)} %ev_h.1) | copy-start | bytes 1572868
  2.7 1.0 %copy-start.2 = (f32[8,128,128]{2,1,0:T(8,128)S(1)}, f32[8,128,128]{2,1,0:T(8,128)}, u32[]{:S(2)}) copy-start(f32[8,128,128]{2,1,0:T(8,128)} %nv_h.1) | copy-start | bytes 1572868
  3.8 1.0 %copy-start.3 = (f32[8,128,128]{2,1,0:T(8,128)S(1)}, f32[8,128,128]{2,1,0:T(8,128)}, u32[]{:S(2)}) copy-start(f32[8,128,128]{2,1,0:T(8,128)} %ts_h.1) | copy-start | bytes 1572868
  4.8 1.0 %copy-start.4 = (f32[8,128,128]{2,1,0:T(8,128)S(1)}, f32[8,128,128]{2,1,0:T(8,128)}, u32[]{:S(2)}) copy-start(f32[8,128,128]{2,1,0:T(8,128)} %ss_h.1) | copy-start | bytes 1572868
  5.8 1.0 %copy-start.5 = (s32[8,128,128]{2,1,0:T(8,128)S(1)}, s32[8,128,128]{2,1,0:T(8,128)}, u32[]{:S(2)}) copy-start(s32[8,128,128]{2,1,0:T(8,128)} %lm_h.1) | copy-start | bytes 1572868
  6.9 0.8 %copy-start.6 = (f32[128,128]{1,0:T(8,128)S(1)}, f32[128,128]{1,0:T(8,128)}, u32[]{:S(2)}) copy-start(f32[128,128]{1,0:T(8,128)} %ha_h.1) | copy-start | bytes 196612
  7.7 0.8 %copy-start.7 = (f32[128,128]{1,0:T(8,128)S(1)}, f32[128,128]{1,0:T(8,128)}, u32[]{:S(2)}) copy-start(f32[128,128]{1,0:T(8,128)} %od_h.1) | copy-start | bytes 196612
  8.6 0.7 %copy-start.8 = (s32[1,1,8]{2,1,0:T(1,128)S(1)}, s32[1,1,8]{2,1,0:T(1,128)}, u32[]{:S(2)}) copy-start(s32[1,1,8]{2,1,0:T(1,128)} %slot_ref.1) | copy-start | bytes 100

commit v2 on v1

--- a/solution.py
+++ b/solution.py
@@ -17,8 +17,9 @@
 CABBELING = 0.3
 HALINE = 0.8
 ITERS = 6
-SCALE = 16.0
+SPAN = 8.0
 G = 8
+FIRST = 6
 LEV, CY, CX = 8, 128, 128
 ROWS, COLS = CY + 2 * G, 2 * CX
 SIZES = {"xl": 2, "z": 8, "c": 2, "xh": 2, "y": 4}
@@ -76,20 +77,23 @@
     return [o for o in itertools.product(*[range(SIZES[d]) for d in stage]) if any(o)]
 
 
-def tree(x):
-    while x.shape[0] > 8:
-        h = x.shape[0] // 2
-        x = x[:h] + x[h:]
-    return x
+def folded(x):
+    h = x.shape[0] // 2
+    hi, lo = two_sum(x[:h], x[h:])
+    while h > 8:
+        h //= 2
+        s, e = two_sum(hi[:h], hi[h:])
+        hi, lo = s, lo[:h] + lo[h:] + e
+    return hi, lo
 
 
 def kernel(
-    slot_ref, ta_h, ha_h, ev_h, nv_h, ts_h, ss_h, lm_h, od_h,
-    tb_h, sb_h, sa_h,
-    ta, ha, ev, nv, store, lm, od,
-    stage, fetched, back, out, edge, edge_in, rows_out, rows_in, corner_in,
-    zed, zed_in, zrow, zrow_in, field, depth, wgt, basis, mail, mail_in, sol,
-    load_sem, bulk_sem, halo_sem, zed_sem, mail_sem, out_sem,
+    slot_h, ta_h, ha_h, ev_h, nv_h, ts_h, ss_h, lm_h, od_h,
+    out, sol,
+    ta, ha, ev, nv, store, lm, od, slot_ref,
+    stage, fetched, back, edge, edge_in, rows_out, rows_in, corner_in,
+    zed, zed_in, zrow, zrow_in, field, depth, wgt, basis, mail, mail_in,
+    load_sem, bulk_sem, halo_sem, zed_sem, mail_sem,
 ):
     gx, gy = lax.axis_index("gx"), lax.axis_index("gy")
     co = {"xl": gx // 16, "z": (gx // 2) % 8, "c": gx % 2, "xh": gy // 4, "y": gy % 4}
@@ -106,7 +110,7 @@
 
     local = [
         (od_h, od), (lm_h.at[0], lm.at[0]), (ha_h, ha),
-        (ts_h, store.at[0]), (ss_h, store.at[1]),
+        (slot_h, slot_ref), (ts_h, store.at[0]), (ss_h, store.at[1]),
         (lm_h.at[pl.ds(1, LEV - 1)], lm.at[pl.ds(1, LEV - 1)]),
         (ta_h, ta), (ev_h, ev), (nv_h, nv),
     ]
@@ -141,7 +145,7 @@
     rows_out[1, 0] = target[120:]
     rows_out[1, 1] = dm[120:]
 
-    for c in loads[3:5]:
+    for c in loads[3:6]:
         c.wait()
     for k in range(LEV):
         slot = slot_ref[0, 0, k]
@@ -166,13 +170,14 @@
         c = pltpu.make_async_remote_copy(a, b, halo_sem.at[0, i], halo_sem.at[1, i], device_id=who)
         c.start()
         halos.append(c)
-    bulks = []
-    for k in range(LEV):
-        c = pltpu.make_async_remote_copy(
+    bulks = [
+        pltpu.make_async_remote_copy(
             stage.at[:, k], fetched.at[:, k], bulk_sem.at[0, k], bulk_sem.at[1, k], device_id=partner
         )
-        c.start()
-        bulks.append(c)
+        for k in range(LEV)
+    ]
+    for c in bulks[:FIRST]:
+        c.start()
 
     for c in halos:
         c.wait_recv()
@@ -202,31 +207,31 @@
     depth[bottom, own] = rows_in[1, 1] * has_south
 
     d = depth[...]
-    for i, (shift, axis) in enumerate(((1, 1), (COLS - 1, 1), (1, 0), (ROWS - 1, 0))):
+    for i, (shift, axis) in enumerate(((COLS - 1, 1), (ROWS - 1, 0))):
         e = pltpu.roll(d, shift, axis)
-        wgt[i] = jnp.where((d > 0.0) & (e > 0.0), (STIFFNESS * 0.5 / SCALE) * (d + e), 0.0)
+        wgt[i] = jnp.where((d > 0.0) & (e > 0.0), (STIFFNESS / SPAN * 2.0) * (d + e), 0.0)
 
     def apply(v):
-        return (
-            wgt[0] * (v - pltpu.roll(v, 1, 1))
-            + wgt[1] * (v - pltpu.roll(v, COLS - 1, 1))
-            + wgt[2] * (v - pltpu.roll(v, 1, 0))
-            + wgt[3] * (v - pltpu.roll(v, ROWS - 1, 0))
-        )
+        fe = wgt[0] * (v - pltpu.roll(v, COLS - 1, 1))
+        fn = wgt[1] * (v - pltpu.roll(v, ROWS - 1, 0))
+        return (fe - pltpu.roll(fe, 1, 1)) + (fn - pltpu.roll(fn, 1, 0))
 
     partial = []
-    v = field[...]
+    v, before = field[...], None
     for k in range(ITERS):
-        nxt = apply(v)
+        image = apply(v)
         if k == 0:
-            basis[...] = nxt
+            basis[...] = image
+            nxt = 0.5 * image - v
+        else:
+            nxt = (image - 2.0 * v) - before
         here, there = v[G : G + CY, :CX], nxt[G : G + CY, :CX]
-        partial.append(tree(here * here))
-        partial.append(tree(here * there))
-        v = nxt
+        partial.append(folded(here * here))
+        partial.append(folded(here * there))
+        v, before = nxt, v
     nm = len(partial)
-    hi = jnp.stack(partial)
-    lo = jnp.zeros_like(hi)
+    hi = jnp.stack([x[0] for x in partial])
+    lo = jnp.stack([x[1] for x in partial])
     for s in (4, 2, 1):
         hi, lo = df_add((hi, lo), (pltpu.roll(hi, s, 1), pltpu.roll(lo, s, 1)))
     sub8 = lax.broadcasted_iota(jnp.int32, (8, CX), 0)
@@ -267,7 +272,7 @@
 
     post(0)
 
-    for c in loads[5:]:
+    for c in loads[6:]:
         c.wait()
     z = jnp.zeros((CY, CX), F32)
     zn = jnp.zeros((8, CX), F32)
@@ -304,19 +309,21 @@
     letter = jnp.where(lane8 < 64, total[0], pltpu.roll(total[1], 64, 1))
     post(1)
 
-    for c in zeds:
-        c.wait_recv()
-    ze, zw = zed_in[0], zed_in[1]
-    for k in range(LEV):
-        b = back[k]
-        b = b + jnp.where(lane == 0, pltpu.roll(zw, 8 - k, 1), 0.0)
-        b = b + jnp.where(lane == CX - 1, pltpu.roll(ze, 127 - k, 1), 0.0)
-        b = b + jnp.where(row == 0, zrow_in[1, pl.ds(k, 1)] * has_south, 0.0)
-        back[k] = b + jnp.where(row == CY - 1, zrow_in[0, pl.ds(k, 1)] * has_north, 0.0)
+    for c in bulks[FIRST:]:
+        c.start()
 
     total = collect(1)
     cur = tuple(jnp.concatenate([t, pltpu.roll(t, 96, 1)], axis=0) for t in total)
-    prev = (jnp.zeros_like(cur[0]), jnp.zeros_like(cur[0]))
+    order = lax.broadcasted_iota(jnp.int32, cur[0].shape, 0)
+    later = order >= 2
+    base = [jnp.where(later, jnp.where(order % 2 == 0, x[:1], x[1:2]), 0.0) for x in cur]
+    cur = df_add([jnp.where(later, 2.0 * x, x) for x in cur], [-x for x in base])
+    shrink = jnp.ones(cur[0].shape, F32)
+    for k in range(2, 2 * ITERS):
+        shrink = jnp.where(order >= k, 0.5 * shrink, shrink)
+    cur = (cur[0] * shrink, cur[1] * shrink)
+    couple = jnp.where(order == 1, 0.5, 0.25)
+    prev = None
 
     def pick(x, k):
         return x[0][k : k + 1], x[1][k : k + 1]
@@ -326,12 +333,15 @@
 
     def up(x):
         return pltpu.roll(x[0], 15, 0), pltpu.roll(x[1], 15, 0)
+
+    def down(x):
+        return couple * pltpu.roll(x[0], 1, 0), couple * pltpu.roll(x[1], 1, 0)
 
     norm = pick(cur, 0)
     ratio = df_div(pick(cur, 1), norm)
     ja, jb = [ratio], []
     for k in range(1, ITERS):
-        nxt = df_add(up(cur), df_neg(df_mul(spread(ja[-1]), cur)))
+        nxt = df_add(df_add(up(cur), down(cur)), df_neg(df_mul(spread(ja[-1]), cur)))
         if k > 1:
             nxt = df_add(nxt, df_neg(df_mul(spread(jb[-1]), prev)))
         fresh = pick(nxt, k)
@@ -341,9 +351,9 @@
         norm, ratio, prev, cur = fresh, new_ratio, cur, nxt
     steps, growths = [], []
     for k in range(ITERS):
-        diag = 1.0 + SCALE * (ja[k][0] + ja[k][1])
+        diag = 1.0 + (SPAN / 2.0) * ((1.0 + ja[k][0]) + ja[k][1])
         if k:
-            off = (SCALE * SCALE) * (jb[k - 1][0] + jb[k - 1][1])
+            off = (SPAN * SPAN / 4.0) * (jb[k - 1][0] + jb[k - 1][1])
             growths.append(off * steps[-1] * steps[-1])
             diag = diag - off * steps[-1]
         steps.append(1.0 / diag)
@@ -357,35 +367,43 @@
     for k in range(ITERS):
         s = s + steps[k] * p
         if k + 1 < ITERS:
-            q = p + SCALE * (basis[...] if k == 0 else apply(p))
+            q = p + (SPAN / 4.0) * (basis[...] if k == 0 else apply(p))
             r = r - steps[k] * q
             p = r + growths[k] * p
     load = depth[...] * s
-    pull = jnp.zeros_like(load)
-    for i, (shift, axis) in enumerate(((1, 1), (COLS - 1, 1), (1, 0), (ROWS - 1, 0))):
-        pull = pull + jnp.where(wgt[i] > 0.0, pltpu.roll(load, shift, axis) - load, 0.0)
+    flow_e = jnp.where(wgt[0] > 0.0, pltpu.roll(load, COLS - 1, 1) - load, 0.0)
+    flow_n = jnp.where(wgt[1] > 0.0, pltpu.roll(load, ROWS - 1, 0) - load, 0.0)
+    pull = (flow_e - pltpu.roll(flow_e, 1, 1)) + (flow_n - pltpu.roll(flow_n, 1, 0))
     sol[...] = s[G : G + CY, :CX]
-    sol_copy = pltpu.make_async_copy(sol, sa_h, out_sem.at[2, 0])
-    sol_copy.start()
     pressure = -GRAVITY * pull[G : G + CY, :CX]
-
-    outs = []
+    for c in zeds:
+        c.wait_recv()
+    ze, zw = zed_in[0], zed_in[1]
     for k in range(LEV):
+        b = back[k]
+        b = b + jnp.where(lane == 0, pltpu.roll(zw, 8 - k, 1), 0.0)
+        b = b + jnp.where(lane == CX - 1, pltpu.roll(ze, 127 - k, 1), 0.0)
+        b = b + jnp.where(row == 0, zrow_in[1, pl.ds(k, 1)] * has_south, 0.0)
+        b = b + jnp.where(row == CY - 1, zrow_in[0, pl.ds(k, 1)] * has_north, 0.0)
+        dens = ((1.0 + k / LEV) * pressure) * lm[k].astype(F32)
         bulks[k].wait_recv()
-        dens = ((1.0 + k / LEV) * pressure) * lm[k].astype(F32)
         ct, cs = fetched[0, k], fetched[1, k]
-        out[0, k] = back[k] + (THERMAL + 2.0 * NONLINEAR * ct + CABBELING * cs) * dens
+        out[0, k] = b + (THERMAL + 2.0 * NONLINEAR * ct + CABBELING * cs) * dens
         out[1, k] = (HALINE + CABBELING * ct) * dens
-        for i, dst in enumerate((tb_h, sb_h)):
-            c = pltpu.make_async_copy(out.at[i, k], dst.at[k], out_sem.at[i, k])
-            c.start()
-            outs.append(c)
     for c in halos + bulks + zeds:
         c.wait_send()
     for st in range(2):
         pltpu.make_async_copy(mail_in.at[st], mail_in.at[st], mail_sem.at[0, st]).wait()
-    sol_copy.wait()
-    for c in outs:
+
+
+def deliver(both, sol, tb_h, sb_h, sa_h, sem):
+    copies = [
+        pltpu.make_async_copy(a, b, sem.at[i])
+        for i, (a, b) in enumerate(((both.at[0], tb_h), (both.at[1], sb_h), (sol, sa_h)))
+    ]
+    for c in copies:
+        c.start()
+    for c in copies:
         c.wait()
 
 
@@ -394,31 +412,41 @@
     cube = (LEV, CY, CX)
     dma = lambda *shape: pltpu.SemaphoreType.DMA(shape)
     n = len(peers(STAGES[0]))
-    hbm = pl.BlockSpec(memory_space=pl.ANY)
+    hbm = pl.BlockSpec(memory_space=pltpu.HBM)
+    vmem = pl.BlockSpec(memory_space=pltpu.VMEM)
+    both, sol = pl.pallas_call(
+        kernel,
+        out_shape=(jax.ShapeDtypeStruct((2,) + cube, F32), jax.ShapeDtypeStruct((CY, CX), F32)),
+        in_specs=[hbm] * 9,
+        out_specs=(vmem, vmem),
+        scratch_shapes=[
+            vm(*cube), vm(CY, CX), vm(*cube), vm(*cube), vm(2, *cube), pltpu.VMEM(cube, jnp.int32), vm(CY, CX),
+            pltpu.SMEM((1, 1, LEV), jnp.int32),
+            vm(2, *cube), vm(2, *cube), vm(*cube),
+            vm(CY, CX), vm(2, CY, CX), vm(2, 2, 8, CX), vm(2, 2, 8, CX), vm(4, 8, CX),
+            vm(CY, CX), vm(2, CY, CX), vm(2, 8, CX), vm(2, 8, CX),
+            vm(ROWS, COLS), vm(ROWS, COLS), vm(2, ROWS, COLS), vm(ROWS, COLS),
+            vm(2, 8, CX), vm(2, n, 8, CX),
+            dma(10), dma(2, LEV), dma(2, 8), dma(2, 4), dma(2, 2),
+        ],
+        compiler_params=pltpu.CompilerParams(
+            collective_id=0, has_side_effects=True, vmem_limit_bytes=40 << 20
+        ),
+        cost_estimate=pl.CostEstimate(flops=40000000, bytes_accessed=60000000, transcendentals=0),
+        name="adjoint",
+    )(*[pltpu.with_memory_space_constraint(x, pltpu.HBM) for x in (slots, ta, ha, ev, nv, ts, ss, lm, od)])
     return pl.pallas_call(
-        kernel,
+        deliver,
         out_shape=(
             jax.ShapeDtypeStruct(cube, F32),
             jax.ShapeDtypeStruct(cube, F32),
             jax.ShapeDtypeStruct((CY, CX), F32),
         ),
-        in_specs=[pl.BlockSpec(memory_space=pltpu.SMEM)] + [hbm] * 8,
+        in_specs=[vmem, vmem],
         out_specs=(hbm, hbm, hbm),
-        scratch_shapes=[
-            vm(*cube), vm(CY, CX), vm(*cube), vm(*cube), vm(2, *cube), pltpu.VMEM(cube, jnp.int32), vm(CY, CX),
-            vm(2, *cube), vm(2, *cube), vm(*cube), vm(2, *cube),
-            vm(CY, CX), vm(2, CY, CX), vm(2, 2, 8, CX), vm(2, 2, 8, CX), vm(4, 8, CX),
-            vm(CY, CX), vm(2, CY, CX), vm(2, 8, CX), vm(2, 8, CX),
-            vm(ROWS, COLS), vm(ROWS, COLS), vm(4, ROWS, COLS), vm(ROWS, COLS),
-            vm(2, 8, CX), vm(2, n, 8, CX), vm(CY, CX),
-            dma(9), dma(2, LEV), dma(2, 8), dma(2, 4), dma(2, 2), dma(3, LEV),
-        ],
-        compiler_params=pltpu.CompilerParams(
-            collective_id=0, has_side_effects=True, vmem_limit_bytes=40 << 20
-        ),
-        cost_estimate=pl.CostEstimate(flops=20000000, bytes_accessed=5000000, transcendentals=0),
-        name="adjoint",
-    )(slots, ta, ha, ev, nv, ts, ss, lm, od)
+        scratch_shapes=[dma(3)],
+        name="deliver",
+    )(*[pltpu.with_memory_space_constraint(x, pltpu.VMEM) for x in (both, sol)])
 
 
 def solution(mesh):

time: 56.7 us -> 38.5 us (0.68)
  local copies, waits for them, and re-layouts: 10.8 us -> 0 us
  Pallas kernels: 44.8 us -> 37.8 us
    unnamed x21 -> x0, local copies, waits for them, and re-layouts: 10.8 us -> none
    pallas_call x1 -> x2, Pallas kernels: 44.8 us -> 37.8 us  [the longest x1 36.8 us: body(): pl.pallas_call(kernel, out_shape=(jax.ShapeDtypeStruct((2,) + cube, F32),...]
where the time goes in v2:
time: 38.5 us; the launch traced here: 38.4 us
  Pallas kernels  37.8 us (98%)
  between operations  0.64 us (2%)
    pallas_call x1, Pallas kernels, body(): pl.pallas_call(kernel, out_shape=(jax.ShapeDtypeStruct((2,) + cube, F32),...  36.8 us
    pallas_call x1, Pallas kernels, body(): pl.pallas_call(deliver, out_shape=(jax.ShapeDtypeStruct(cube, F32), jax.S...  1 us

profile of v2, /device:TPU:1, one launch (start us, length us, event | category | flops | bytes accessed | tf_op | source)
XLA Modules:
  0.0 38.4 jit_solution(17868646067702739877)
XLA Ops:
  0.6 36.8 %adjoint.1 = (f32[2,8,128,128]{3,2,1,0:T(8,128)S(1)}, f32[128,128]{1,0:T(8,128)S(1)}) custom-call(s32[1,1,8]{2,1,0:T(1,128)} %slot_h.1, f32[8,128,128]{2,1,0:T(8,128)} %ta_h.1, f32[128,128]{1,0:T(8,128)} %ha_h.1, f32[8,128,128]{2,1,0:T(8,128)} %ev_h.1, f32[8,128,128]{2,1,0:T(8,128)} %nv_h.1, f32[8,128,128]{2,1,0:T(8,128)} %ts_h.1, f32[8,128,128]{2,1,0:T(8,128)} %ss_h.1, ...), custom_call_target="tpu_custom_call" | custom-call | flops 40000000 | bytes 60000000 | tf_op jit(solution)/shard_map/adjoint/pallas_call | solution.py:417
  37.4 1.0 %deliver.1 = (f32[8,128,128]{2,1,0:T(8,128)}, f32[8,128,128]{2,1,0:T(8,128)}, f32[128,128]{1,0:T(8,128)}) custom-call(f32[2,8,128,128]{3,2,1,0:T(8,128)S(1)} %get-tuple-element.5.both, f32[128,128]{1,0:T(8,128)S(1)} %get-tuple-element.6.sol), custom_call_target="tpu_custom_call" | custom-call | tf_op jit(solution)/shard_map/deliver/pallas_call | solution.py:438

commit v3 on v2

--- a/solution.py
+++ b/solution.py
@@ -19,11 +19,12 @@
 ITERS = 6
 SPAN = 8.0
 G = 8
-FIRST = 6
+BATCH = (4, 0, 0, 0, 1)
 LEV, CY, CX = 8, 128, 128
 ROWS, COLS = CY + 2 * G, 2 * CX
 SIZES = {"xl": 2, "z": 8, "c": 2, "xh": 2, "y": 4}
 STAGES = (("z", "c"), ("xl", "xh", "y"))
+HOPS = {"xl": 1.0, "z": 1.0, "c": 0.3, "xh": 2.0, "y": 1.0}
 F32 = jnp.float32
 
 
@@ -74,7 +75,8 @@
 
 
 def peers(stage):
-    return [o for o in itertools.product(*[range(SIZES[d]) for d in stage]) if any(o)]
+    offs = [o for o in itertools.product(*[range(SIZES[d]) for d in stage]) if any(o)]
+    return sorted(offs, key=lambda o: -sum(HOPS[d] * min(k, SIZES[d] - k) for d, k in zip(stage, o)))
 
 
 def folded(x):
@@ -93,7 +95,7 @@
     ta, ha, ev, nv, store, lm, od, slot_ref,
     stage, fetched, back, edge, edge_in, rows_out, rows_in, corner_in,
     zed, zed_in, zrow, zrow_in, field, depth, wgt, basis, mail, mail_in,
-    load_sem, bulk_sem, halo_sem, zed_sem, mail_sem,
+    load_sem, bulk_sem, halo_sem, zed_sem, mail_sem, ready_sem,
 ):
     gx, gy = lax.axis_index("gx"), lax.axis_index("gy")
     co = {"xl": gx // 16, "z": (gx // 2) % 8, "c": gx % 2, "xh": gy // 4, "y": gy % 4}
@@ -119,7 +121,8 @@
         c.start()
 
     barrier = pltpu.get_barrier_semaphore()
-    greeted = [peer(st, off) for st in STAGES for off in peers(st)]
+    greeted = [peer(STAGES[1], off) for off in peers(STAGES[1])]
+    greeted += [peer(STAGES[0], off) for off in ((1, 0), (1, 1), (7, 0), (7, 1))]
     greeted += [(a, b) for a in (west, east) for b in (south, gy, north)]
     for who in greeted:
         pl.semaphore_signal(barrier, inc=1, device_id=who)
@@ -176,11 +179,30 @@
         )
         for k in range(LEV)
     ]
-    for c in bulks[:FIRST]:
-        c.start()
-
-    for c in halos:
-        c.wait_recv()
+    def ready(step):
+        for i, off in enumerate((step, 8 - step)):
+            pl.semaphore_signal(ready_sem.at[step - 1, i], inc=1, device_id=peer(("z",), (off,)))
+
+    def await_ready(step):
+        for i in range(2):
+            pl.semaphore_wait(ready_sem.at[step - 1, i], 1)
+
+    ready(1)
+    queue = list(bulks)
+
+    def feed(count):
+        for c in queue[:count]:
+            c.start()
+        del queue[:count]
+
+    feed(BATCH[0])
+    for group, count in zip((halos[:2], halos[2:4], halos[4:]), BATCH[1:4]):
+        for c in group:
+            c.wait_recv()
+        feed(count)
+        if group[0] is halos[0]:
+            await_ready(1)
+            ready(2)
     has_north = jnp.where(gy < 7, 1.0, 0.0).astype(F32)
     has_south = jnp.where(gy > 0, 1.0, 0.0).astype(F32)
 
@@ -270,7 +292,9 @@
             terms = [df_add(terms[i], terms[i + 1]) for i in range(0, len(terms), 2)]
         return terms[0]
 
+    await_ready(2)
     post(0)
+    feed(BATCH[4])
 
     for c in loads[6:]:
         c.wait()
@@ -308,9 +332,7 @@
     total = collect(0)
     letter = jnp.where(lane8 < 64, total[0], pltpu.roll(total[1], 64, 1))
     post(1)
-
-    for c in bulks[FIRST:]:
-        c.start()
+    feed(LEV)
 
     total = collect(1)
     cur = tuple(jnp.concatenate([t, pltpu.roll(t, 96, 1)], axis=0) for t in total)
@@ -427,7 +449,7 @@
             vm(CY, CX), vm(2, CY, CX), vm(2, 8, CX), vm(2, 8, CX),
             vm(ROWS, COLS), vm(ROWS, COLS), vm(2, ROWS, COLS), vm(ROWS, COLS),
             vm(2, 8, CX), vm(2, n, 8, CX),
-            dma(10), dma(2, LEV), dma(2, 8), dma(2, 4), dma(2, 2),
+            dma(10), dma(2, LEV), dma(2, 8), dma(2, 4), dma(2, 2), pltpu.SemaphoreType.REGULAR((2, 2)),
         ],
         compiler_params=pltpu.CompilerParams(
             collective_id=0, has_side_effects=True, vmem_limit_bytes=40 << 20

time: 38.5 us -> 36.1 us (0.938); the launches traced: 38.4 us -> 35.4 us
  Pallas kernels: 37.8 us -> 34.7 us
    pallas_call x1, Pallas kernels: 36.8 us -> 33.7 us  [body(): pl.pallas_call(kernel, out_shape=(jax.ShapeDtypeStruct((2,) + cube, F32),...]
where the time goes in v3:
time: 36.1 us; the launch traced here: 35.4 us
  Pallas kernels  34.7 us (96%)
  between operations  0.64 us (2%)
    pallas_call x1, Pallas kernels, body(): pl.pallas_call(kernel, out_shape=(jax.ShapeDtypeStruct((2,) + cube, F32),...  33.7 us
    pallas_call x1, Pallas kernels, body(): pl.pallas_call(deliver, out_shape=(jax.ShapeDtypeStruct(cube, F32), jax.S...  1 us

profile of v3, /device:TPU:1, one launch (start us, length us, event | category | flops | bytes accessed | tf_op | source)
XLA Modules:
  0.0 35.4 jit_solution(6400201208709675457)
XLA Ops:
  0.6 33.7 %adjoint.1 = (f32[2,8,128,128]{3,2,1,0:T(8,128)S(1)}, f32[128,128]{1,0:T(8,128)S(1)}) custom-call(s32[1,1,8]{2,1,0:T(1,128)} %slot_h.1, f32[8,128,128]{2,1,0:T(8,128)} %ta_h.1, f32[128,128]{1,0:T(8,128)} %ha_h.1, f32[8,128,128]{2,1,0:T(8,128)} %ev_h.1, f32[8,128,128]{2,1,0:T(8,128)} %nv_h.1, f32[8,128,128]{2,1,0:T(8,128)} %ts_h.1, f32[8,128,128]{2,1,0:T(8,128)} %ss_h.1, ...), custom_call_target="tpu_custom_call" | custom-call | flops 40000000 | bytes 60000000 | tf_op jit(solution)/shard_map/adjoint/pallas_call | solution.py:439
  34.4 1.0 %deliver.1 = (f32[8,128,128]{2,1,0:T(8,128)}, f32[8,128,128]{2,1,0:T(8,128)}, f32[128,128]{1,0:T(8,128)}) custom-call(f32[2,8,128,128]{3,2,1,0:T(8,128)S(1)} %get-tuple-element.5.both, f32[128,128]{1,0:T(8,128)S(1)} %get-tuple-element.6.sol), custom_call_target="tpu_custom_call" | custom-call | tf_op jit(solution)/shard_map/deliver/pallas_call | solution.py:460

commit v4 on v3

--- a/solution.py
+++ b/solution.py
@@ -19,7 +19,7 @@
 ITERS = 6
 SPAN = 8.0
 G = 8
-BATCH = (4, 0, 0, 0, 1)
+BATCH = (5, 0, 0, 0, 0)
 LEV, CY, CX = 8, 128, 128
 ROWS, COLS = CY + 2 * G, 2 * CX
 SIZES = {"xl": 2, "z": 8, "c": 2, "xh": 2, "y": 4}
@@ -110,6 +110,13 @@
     south, north = (gy + 7) % 8, (gy + 1) % 8
     partner = ((gx + 16) % 32, gy)
 
+    barrier = pltpu.get_barrier_semaphore()
+    greeted = [(a, b) for a in (west, east) for b in (south, north, gy)]
+    greeted += [peer(STAGES[1], off) for off in peers(STAGES[1])]
+    greeted += [peer(STAGES[0], off) for off in ((1, 0), (1, 1), (7, 0), (7, 1))]
+    for who in greeted:
+        pl.semaphore_signal(barrier, inc=1, device_id=who)
+
     local = [
         (od_h, od), (lm_h.at[0], lm.at[0]), (ha_h, ha),
         (slot_h, slot_ref), (ts_h, store.at[0]), (ss_h, store.at[1]),
@@ -119,13 +126,6 @@
     loads = [pltpu.make_async_copy(a, b, load_sem.at[i]) for i, (a, b) in enumerate(local)]
     for c in loads:
         c.start()
-
-    barrier = pltpu.get_barrier_semaphore()
-    greeted = [peer(STAGES[1], off) for off in peers(STAGES[1])]
-    greeted += [peer(STAGES[0], off) for off in ((1, 0), (1, 1), (7, 0), (7, 1))]
-    greeted += [(a, b) for a in (west, east) for b in (south, gy, north)]
-    for who in greeted:
-        pl.semaphore_signal(barrier, inc=1, device_id=who)
 
     lane = lax.broadcasted_iota(jnp.int32, (CY, CX), 1)
     row = lax.broadcasted_iota(jnp.int32, (CY, CX), 0)

time: 36.1 us -> 36 us (level)
  no operation moved by 1% of the time
where the time goes in v4:
time: 36 us; the launch traced here: 35.4 us
  Pallas kernels  34.8 us (97%)
  between operations  0.64 us (2%)
    pallas_call x1, Pallas kernels, body(): pl.pallas_call(kernel, out_shape=(jax.ShapeDtypeStruct((2,) + cube, F32),...  33.8 us
    pallas_call x1, Pallas kernels, body(): pl.pallas_call(deliver, out_shape=(jax.ShapeDtypeStruct(cube, F32), jax.S...  1 us

profile of v4, /device:TPU:1, one launch (start us, length us, event | category | flops | bytes accessed | tf_op | source)
XLA Modules:
  0.0 35.4 jit_solution(14140788025039546714)
XLA Ops:
  0.6 33.8 %adjoint.1 = (f32[2,8,128,128]{3,2,1,0:T(8,128)S(1)}, f32[128,128]{1,0:T(8,128)S(1)}) custom-call(s32[1,1,8]{2,1,0:T(1,128)} %slot_h.1, f32[8,128,128]{2,1,0:T(8,128)} %ta_h.1, f32[128,128]{1,0:T(8,128)} %ha_h.1, f32[8,128,128]{2,1,0:T(8,128)} %ev_h.1, f32[8,128,128]{2,1,0:T(8,128)} %nv_h.1, f32[8,128,128]{2,1,0:T(8,128)} %ts_h.1, f32[8,128,128]{2,1,0:T(8,128)} %ss_h.1, ...), custom_call_target="tpu_custom_call" | custom-call | flops 40000000 | bytes 60000000 | tf_op jit(solution)/shard_map/adjoint/pallas_call | solution.py:439
  34.4 1.0 %deliver.1 = (f32[8,128,128]{2,1,0:T(8,128)}, f32[8,128,128]{2,1,0:T(8,128)}, f32[128,128]{1,0:T(8,128)}) custom-call(f32[2,8,128,128]{3,2,1,0:T(8,128)S(1)} %get-tuple-element.5.both, f32[128,128]{1,0:T(8,128)S(1)} %get-tuple-element.6.sol), custom_call_target="tpu_custom_call" | custom-call | tf_op jit(solution)/shard_map/deliver/pallas_call | solution.py:460
